TPU v7x, 32 devices: a whole 2x2x4 slice. The times are simulated.
32 devices in a mesh: mom: 4 (over y, x), sec: 8 (over z, core).
Axes of the slice: x: 2, y: 2, z: 4, core: 2. Of those that a mesh axis runs over, the one named last changes fastest.
Arguments:
- left_env: bfloat16 [64, 64, 2816], P('sec', 'mom'), may hold values from -0.75 to 0.75
- right_env: bfloat16 [64, 64, 2816], P('sec', 'mom'), may hold values from -0.109375 to 0.109375
- left_mixed: bfloat16 [4, 64, 64, 2816], P('mom', 'sec'), may hold values from -0.75 to 0.75
- excitation: bfloat16 [4, 64, 64, 256], P('mom', 'sec'), may hold values from -6 to 6
- ground: bfloat16 [64, 64, 256], P('sec'), may hold values from -6 to 6
- mpo: bfloat16 [44, 4, 44, 4], replicated, may hold values from -0.4375 to 0.4375
- momentum: int32 [4], P('mom'), may hold values from 0 to 3, each once
- block_dims: int32 [64], P('sec'), may hold values from 16 to 64, as said below
Outputs:
- excited: bfloat16 [4, 2, 64, 64, 256], P('mom', None, 'sec')
Inputs may be any that keep to these rules, and one draw needn't show every extreme that they name: `block_dims`: every block has at least 16 used rows; some block uses all 64 and some exactly 16.
All inputs are finite; a program needn't handle non-finite values.
Results may differ from a plain program's by a relative error of at most 0.0058.
Values may be sent and summed in bfloat16 or wider, within the bound.
No kernel may reach another device: no remote copies, remote signals or barrier semaphores. Data moves between devices by JAX's collectives and lax.ppermute only.
A program may use at most 128 MiB of HBM per device.

v0:
```python
import math

import jax
import jax.numpy as jnp
from jax import lax
from jax.sharding import PartitionSpec as P


def with_halo(shard, sides, width):
    for axis, dim in sides:
        devices, length = (lax.axis_size(axis), shard.shape[dim])
        up = [(i, (i + 1) % devices) for i in range(devices - 1)]
        down = [(j, i) for i, j in up]
        last = lax.slice_in_dim(shard, length - width, length, axis=dim)
        initial = lax.slice_in_dim(shard, 0, width, axis=dim)
        before = lax.ppermute(last, axis, up)
        after = lax.ppermute(initial, axis, down)
        shard = jnp.concatenate([before, shard, after], axis=dim)
    return shard


def apply_term(left, source, right, mpo):
    width = left.shape[1]
    low = width // 3
    high = width - low
    bounds = [(0, low), (low, high), (high, width)]
    count = source.shape[0]
    rows = left.shape[0]
    block = right.shape[0]
    wide = source.shape[-1]
    phys = wide // block
    total = None
    for shift in range(3):
        start, stop = bounds[shift]
        temp = jnp.einsum(
            "iwa,nab->niwb",
            left[:, start:stop, :],
            source[:, shift],
            preferred_element_type=jnp.float32,
        ).astype(jnp.bfloat16)
        temp = temp.reshape(count, rows, stop - start, phys, block)
        part_sum = jnp.einsum(
            "niwpj,wpvq->nviqj", temp, mpo[start:stop], preferred_element_type=jnp.float32
        )
        total = part_sum if total is None else total + part_sum
    mixed = total.astype(jnp.bfloat16)
    result = jnp.einsum("nviqj,jvk->niqk", mixed, right, preferred_element_type=jnp.float32)
    return result.reshape(count, rows, wide)


def shards(left_env, right_env, left_mixed, excitation, ground, mpo, momentum, block_dims):
    sectors = excitation.shape[1]
    block = excitation.shape[2]
    wide = excitation.shape[3]
    width = left_env.shape[2] // block
    groups = lax.axis_size("mom")
    right_full = lax.all_gather(right_env, "mom", axis=1, tiled=True)
    stacked = jnp.stack([excitation[0], ground])
    padded = with_halo(stacked, (("sec", 1),), 1)
    sector_ids = jnp.arange(sectors, dtype=jnp.int32)

    def shifted_sector(sector):
        right = right_full[sector].reshape(block, width, block)
        mixl = left_mixed[0, sector].reshape(block, width, block)
        src = lax.dynamic_slice_in_dim(padded[1:2], sector, 3, 1)
        return apply_term(mixl, src, right, mpo)[0]

    shifted = lax.map(shifted_sector, sector_ids)
    left_full = lax.all_gather(left_env, "mom", axis=1, tiled=True)

    def direct_sector(sector):
        right = right_full[sector].reshape(block, width, block)
        left = left_full[sector].reshape(block, width, block)
        src = lax.dynamic_slice_in_dim(padded[0:1], sector, 3, 1)
        return apply_term(left, src, right, mpo)[0]

    direct = lax.map(direct_sector, sector_ids)
    phase = 2.0 * math.pi * momentum[0].astype(jnp.float32) / groups
    rows_idx = jnp.arange(block, dtype=jnp.int32)
    cols_idx = jnp.arange(wide, dtype=jnp.int32) % block
    used = block_dims[:, None, None]
    mask = ((rows_idx[None, :, None] < used) & (cols_idx[None, None, :] < used)).astype(jnp.float32)
    real_part = mask * (direct + jnp.cos(phase) * shifted)
    imag_part = -mask * jnp.sin(phase) * shifted
    return jnp.stack([real_part, imag_part])[None].astype(jnp.bfloat16)


def solution(mesh):
    return jax.shard_map(
        shards,
        mesh=mesh,
        in_specs=(
            P("sec", "mom", None),
            P("sec", "mom", None),
            P("mom", "sec", None, None),
            P("mom", "sec", None, None),
            P("sec", None, None),
            P(),
            P("mom"),
            P("sec"),
        ),
        out_specs=P("mom", None, "sec", None, None),
        check_vma=False,
    )
```

profile of v0, /device:TPU:0, one launch (start us, length us, event | category | flops | bytes accessed | tf_op | source)
XLA Modules:
  0.0 640.0 jit_solution(17581412542030367887)
XLA Ops:
  18.7 35.0 %all-gather.3.cloned.1.call-done = bf16[8,64,2816]{2,1,0:T(8,128)(2,1)} async-done(((bf16[8,16,2816]{2,1,0:T(8,128)(2,1)}), bf16[8,64,2816]{2,1,0:T(8,128)(2,1)}) %all-gather.3.cloned.1.call-update) | async-done | bytes 2883600 | tf_op jit(solution)/shard_map/all_gather | solution.py:69
  53.7 43.7 %all-gather.5.cloned.1.call-done = bf16[8,64,2816]{2,1,0:T(8,128)(2,1)} async-done(((bf16[8,16,2816]{2,1,0:T(8,128)(2,1)}), bf16[8,64,2816]{2,1,0:T(8,128)(2,1)}) %all-gather.5.cloned.1.call-update) | async-done | bytes 2883600 | tf_op jit(solution)/shard_map/all_gather | solution.py:57
  98.3 268.4 %while.20 = (s32[]{:T(128)}, f32[8,64,256]{2,1,0:T(8,128)}, bf16[2,10,64,256]{3,2,1,0:T(8,128)(2,1)S(1)}, s32[8]{0:T(128)S(1)}, bf16[8,64,2816]{2,1,0:T(8,128)(2...) while((s32[]{:T(128)}, f32[8,64,256]{2,1,0:T(8,128)}, ...), condition=%wide.region_1.2_spmd, body=%wide.region_0.1_spmd.sunk | while | flops 441188352 | bytes 44241284 | solution.py:77
  104.7 3.7 fusion.105
  115.9 6.3 fusion.110
  122.3 5.2 copy.125
  138.2 3.7 fusion.105
  143.5 3.7 fusion.108
  149.5 6.3 fusion.110
  155.8 5.2 copy.125
  171.8 3.7 fusion.105
  177.0 3.7 fusion.108
  183.0 6.3 fusion.110
  189.4 5.2 copy.125
  205.3 3.7 fusion.105
  210.6 3.7 fusion.108
  216.6 6.3 fusion.110
  222.9 5.2 copy.125
  238.9 3.7 fusion.105
  244.1 3.7 fusion.108
  250.1 6.3 fusion.110
  256.5 5.2 copy.125
  272.5 3.7 fusion.105
  277.7 3.7 fusion.108
  283.7 6.3 fusion.110
  290.0 5.2 copy.125
  306.0 3.7 fusion.105
  311.2 3.7 fusion.108
  317.3 6.3 fusion.110
  323.6 5.2 copy.125
  339.6 3.7 fusion.105
  344.8 3.7 fusion.108
  350.8 6.3 fusion.110
  357.2 5.2 copy.125
  367.5 263.4 %while.21 = (s32[]{:T(128)}, f32[8,64,256]{2,1,0:T(8,128)}, bf16[2,10,64,256]{3,2,1,0:T(8,128)(2,1)S(1)}, s32[8]{0:T(128)S(1)}, bf16[1,8,64,2816]{3,2,1,0:T(8,12...) while((s32[]{:T(128)}, f32[8,64,256]{2,1,0:T(8,128)}, ...), condition=%wide.region_3.4_spmd, body=%wide.region_2.3_spmd.sunk | while | flops 441188352 | bytes 43225452 | solution.py:68
  373.8 3.7 fusion.123
  378.2 3.7 fusion.126
  383.5 6.3 fusion.128
  389.8 5.2 copy.133
  406.7 3.7 fusion.123
  411.2 3.7 fusion.126
  416.4 6.3 fusion.128
  422.8 5.2 copy.133
  439.6 3.7 fusion.123
  444.1 3.7 fusion.126
  449.3 6.3 fusion.128
  455.7 5.2 copy.133
  472.5 3.7 fusion.123
  482.3 6.3 fusion.128
  488.6 5.2 copy.133
  505.5 3.7 fusion.123
  515.2 6.3 fusion.128
  521.5 5.2 copy.133
  538.4 3.7 fusion.123
  542.9 3.7 fusion.126
  548.1 6.3 fusion.128
  554.5 5.2 copy.133
  571.3 3.7 fusion.123
  581.1 6.3 fusion.128
  587.4 5.2 copy.133
  604.3 3.7 fusion.123
  608.8 3.7 fusion.126
  614.0 6.3 fusion.128
  620.3 5.2 copy.133
  (452 shorter events, 205.8 us)
Async XLA Ops:
  6.5 47.2 %all-gather.3.cloned.1.call-start = ((), (), s32[]{:S(2)}) async-start(), calls=%async_computation | async-start | bytes 3604480 | tf_op jit(solution)/shard_map/all_gather | solution.py:69
  7.3 90.2 %all-gather.5.cloned.1.call-start = ((), (), s32[]{:S(2)}) async-start(), calls=%async_computation.1 | async-start | bytes 3604480 | tf_op jit(solution)/shard_map/all_gather | solution.py:57
  8.8 8.7 %collective-permute-start.1 = (bf16[2,1,64,256]{3,2,1,0:T(8,128)(2,1)S(1)}, bf16[2,1,64,256]{3,2,1,0:T(8,128)(2,1)S(1)}, u32[]{:S(2)}, u32[]{:S(2)}) collective-permute-start(bf16[2,1,64,256]{3,2,1,0:T(8,128)(2,1)S(1)} %get-tuple-element.146), channel_id=1, source_target_pairs={{1,0},{2,1},{3,2},{4,3},{5,4},{6,5},{7,6},{9,8},{10,9},{11,10},{12... | collective-permute-start | bytes 196616 | tf_op jit(solution)/shard_map/ppermute | solution.py:17
  10.1 7.4 %collective-permute-start = (bf16[2,1,64,256]{3,2,1,0:T(8,128)(2,1)S(1)}, bf16[2,1,64,256]{3,2,1,0:T(8,128)(2,1)S(1)}, u32[]{:S(2)}, u32[]{:S(2)}) collective-permute-start(bf16[2,1,64,256]{3,2,1,0:T(8,128)(2,1)S(1)} %get-tuple-element.145), channel_id=1, source_target_pairs={{0,1},{1,2},{2,3},{3,4},{4,5},{5,6},{6,7},{8,9},{9,10},{10,11},{11... | collective-permute-start | bytes 196616 | tf_op jit(solution)/shard_map/ppermute | solution.py:16
  98.3 5.7 copy-start.4
  98.3 11.6 %copy-start = (bf16[44,4,44,4]{2,0,1,3:T(8,128)(2,1)}, bf16[44,4,44,4]{2,0,1,3:T(8,128)(2,1)S(1)}, u32[]{:S(2)}) copy-start(bf16[44,4,44,4]{2,0,1,3:T(8,128)(2,1)S(1)} %get-tuple-element.276) | copy-start | bytes 185860 | tf_op jit(solution)/shard_map/while
  127.5 4.3 copy-start.1
  127.5 4.3 copy-start.5
  131.8 5.7 copy-start.4
  131.8 11.6 %copy-start = (bf16[44,4,44,4]{2,0,1,3:T(8,128)(2,1)}, bf16[44,4,44,4]{2,0,1,3:T(8,128)(2,1)S(1)}, u32[]{:S(2)}) copy-start(bf16[44,4,44,4]{2,0,1,3:T(8,128)(2,1)S(1)} %get-tuple-element.276) | copy-start | bytes 185860 | tf_op jit(solution)/shard_map/while
  161.0 4.3 copy-start.1
  161.0 4.3 copy-start.5
  165.4 5.7 copy-start.4
  165.4 11.6 %copy-start = (bf16[44,4,44,4]{2,0,1,3:T(8,128)(2,1)}, bf16[44,4,44,4]{2,0,1,3:T(8,128)(2,1)S(1)}, u32[]{:S(2)}) copy-start(bf16[44,4,44,4]{2,0,1,3:T(8,128)(2,1)S(1)} %get-tuple-element.276) | copy-start | bytes 185860 | tf_op jit(solution)/shard_map/while
  194.6 4.3 copy-start.1
  194.6 4.3 copy-start.5
  198.9 5.7 copy-start.4
  198.9 11.6 %copy-start = (bf16[44,4,44,4]{2,0,1,3:T(8,128)(2,1)}, bf16[44,4,44,4]{2,0,1,3:T(8,128)(2,1)S(1)}, u32[]{:S(2)}) copy-start(bf16[44,4,44,4]{2,0,1,3:T(8,128)(2,1)S(1)} %get-tuple-element.276) | copy-start | bytes 185860 | tf_op jit(solution)/shard_map/while
  228.2 4.3 copy-start.1
  228.2 4.3 copy-start.5
  232.5 5.7 copy-start.4
  232.5 11.6 %copy-start = (bf16[44,4,44,4]{2,0,1,3:T(8,128)(2,1)}, bf16[44,4,44,4]{2,0,1,3:T(8,128)(2,1)S(1)}, u32[]{:S(2)}) copy-start(bf16[44,4,44,4]{2,0,1,3:T(8,128)(2,1)S(1)} %get-tuple-element.276) | copy-start | bytes 185860 | tf_op jit(solution)/shard_map/while
  261.7 4.3 copy-start.5
  266.0 5.7 copy-start.4
  266.0 11.6 %copy-start = (bf16[44,4,44,4]{2,0,1,3:T(8,128)(2,1)}, bf16[44,4,44,4]{2,0,1,3:T(8,128)(2,1)S(1)}, u32[]{:S(2)}) copy-start(bf16[44,4,44,4]{2,0,1,3:T(8,128)(2,1)S(1)} %get-tuple-element.276) | copy-start | bytes 185860 | tf_op jit(solution)/shard_map/while
  295.3 4.3 copy-start.5
  299.6 5.7 copy-start.4
  299.6 11.6 %copy-start = (bf16[44,4,44,4]{2,0,1,3:T(8,128)(2,1)}, bf16[44,4,44,4]{2,0,1,3:T(8,128)(2,1)S(1)}, u32[]{:S(2)}) copy-start(bf16[44,4,44,4]{2,0,1,3:T(8,128)(2,1)S(1)} %get-tuple-element.276) | copy-start | bytes 185860 | tf_op jit(solution)/shard_map/while
  328.8 4.3 copy-start.1
  328.8 4.3 copy-start.5
  333.1 5.7 copy-start.4
  333.2 11.6 %copy-start = (bf16[44,4,44,4]{2,0,1,3:T(8,128)(2,1)}, bf16[44,4,44,4]{2,0,1,3:T(8,128)(2,1)S(1)}, u32[]{:S(2)}) copy-start(bf16[44,4,44,4]{2,0,1,3:T(8,128)(2,1)S(1)} %get-tuple-element.276) | copy-start | bytes 185860 | tf_op jit(solution)/shard_map/while
  362.4 4.3 copy-start.1
  362.4 4.3 copy-start.5
  367.5 263.4 %copy-start.9 = (pred[8,256]{1,0:T(8,128)(4,1)S(1)}, pred[8,256]{1,0:T(8,128)(4,1)}, u32[]{:S(2)}) copy-start(pred[8,256]{1,0:T(8,128)(4,1)} %broadcast_compare_fusion) | copy-start | bytes 6148
  367.5 263.4 %copy-start.10 = (pred[8,64]{1,0:T(8,128)(4,1)S(1)}, pred[8,64]{1,0:T(8,128)(4,1)}, u32[]{:S(2)}) copy-start(pred[8,64]{1,0:T(8,128)(4,1)} %iota_compare_fusion) | copy-start | bytes 1540
  367.5 5.5 copy-start.6
  367.5 10.7 %copy-start.2 = (bf16[44,4,44,4]{2,0,1,3:T(8,128)(2,1)}, bf16[44,4,44,4]{2,0,1,3:T(8,128)(2,1)S(1)}, u32[]{:S(2)}) copy-start(bf16[44,4,44,4]{2,0,1,3:T(8,128)(2,1)S(1)} %get-tuple-element.315) | copy-start | bytes 185860 | tf_op jit(solution)/shard_map/while
  396.1 4.3 copy-start.3
  400.4 5.6 copy-start.6
  400.4 10.8 %copy-start.2 = (bf16[44,4,44,4]{2,0,1,3:T(8,128)(2,1)}, bf16[44,4,44,4]{2,0,1,3:T(8,128)(2,1)S(1)}, u32[]{:S(2)}) copy-start(bf16[44,4,44,4]{2,0,1,3:T(8,128)(2,1)S(1)} %get-tuple-element.315) | copy-start | bytes 185860 | tf_op jit(solution)/shard_map/while
  429.0 4.3 copy-start.3
  433.3 5.6 copy-start.6
  433.3 10.8 %copy-start.2 = (bf16[44,4,44,4]{2,0,1,3:T(8,128)(2,1)}, bf16[44,4,44,4]{2,0,1,3:T(8,128)(2,1)S(1)}, u32[]{:S(2)}) copy-start(bf16[44,4,44,4]{2,0,1,3:T(8,128)(2,1)S(1)} %get-tuple-element.315) | copy-start | bytes 185860 | tf_op jit(solution)/shard_map/while
  461.9 4.3 copy-start.3
  466.2 5.6 copy-start.6
  466.2 10.8 %copy-start.2 = (bf16[44,4,44,4]{2,0,1,3:T(8,128)(2,1)}, bf16[44,4,44,4]{2,0,1,3:T(8,128)(2,1)S(1)}, u32[]{:S(2)}) copy-start(bf16[44,4,44,4]{2,0,1,3:T(8,128)(2,1)S(1)} %get-tuple-element.315) | copy-start | bytes 185860 | tf_op jit(solution)/shard_map/while
  494.8 4.3 copy-start.3
  499.2 5.6 copy-start.6
  499.2 10.8 %copy-start.2 = (bf16[44,4,44,4]{2,0,1,3:T(8,128)(2,1)}, bf16[44,4,44,4]{2,0,1,3:T(8,128)(2,1)S(1)}, u32[]{:S(2)}) copy-start(bf16[44,4,44,4]{2,0,1,3:T(8,128)(2,1)S(1)} %get-tuple-element.315) | copy-start | bytes 185860 | tf_op jit(solution)/shard_map/while
  527.8 4.3 copy-start.3
  527.8 4.3 copy-start.7
  532.1 5.6 copy-start.6
  532.1 10.8 %copy-start.2 = (bf16[44,4,44,4]{2,0,1,3:T(8,128)(2,1)}, bf16[44,4,44,4]{2,0,1,3:T(8,128)(2,1)S(1)}, u32[]{:S(2)}) copy-start(bf16[44,4,44,4]{2,0,1,3:T(8,128)(2,1)S(1)} %get-tuple-element.315) | copy-start | bytes 185860 | tf_op jit(solution)/shard_map/while
  560.7 4.3 copy-start.3
  560.7 4.3 copy-start.7
  565.0 5.6 copy-start.6
  565.0 10.8 %copy-start.2 = (bf16[44,4,44,4]{2,0,1,3:T(8,128)(2,1)}, bf16[44,4,44,4]{2,0,1,3:T(8,128)(2,1)S(1)}, u32[]{:S(2)}) copy-start(bf16[44,4,44,4]{2,0,1,3:T(8,128)(2,1)S(1)} %get-tuple-element.315) | copy-start | bytes 185860 | tf_op jit(solution)/shard_map/while
  593.7 4.3 copy-start.3
  593.7 4.3 copy-start.7
  598.0 5.6 copy-start.6
  598.0 10.8 %copy-start.2 = (bf16[44,4,44,4]{2,0,1,3:T(8,128)(2,1)}, bf16[44,4,44,4]{2,0,1,3:T(8,128)(2,1)S(1)}, u32[]{:S(2)}) copy-start(bf16[44,4,44,4]{2,0,1,3:T(8,128)(2,1)S(1)} %get-tuple-element.315) | copy-start | bytes 185860 | tf_op jit(solution)/shard_map/while
  626.6 4.3 copy-start.3
  626.6 4.3 copy-start.7
  (14 other events, 41.6 us)
Sparse Core Ops, SparseCore 0:
  9.2 44.4 all-gather.2
  55.6 41.7 all-gather.4
where the time goes:
time: 643 us; the launch traced here: 640 us
  matrix products  291 us (45%)
  local copies, waits for them, and re-layouts  191 us (30%)
  waiting for transfers between devices  80.1 us (12%)
  loops' own time  52.6 us (8%)
  between operations  14.3 us (2%)
  other arithmetic  6.82 us (1%)
    dot_general x48, matrix products, apply_term(): jnp.einsum('niwpj,wpvq->nviqj', temp, mpo[start:stop], preferred_element_...  220 us
    another operation x66, local copies, waits for them, and re-layouts  119 us
    dot_general x16, matrix products, apply_term(): jnp.einsum('nviqj,jvk->niqk', mixed, right, preferred_element_type=jnp.fl...  46.1 us
    all_gather x1, waiting for transfers between devices, shards(): right_full = lax.all_gather(right_env, 'mom', axis=1, tiled=True)  43.7 us
    all_gather x1, waiting for transfers between devices, shards(): left_full = lax.all_gather(left_env, 'mom', axis=1, tiled=True)  35 us
    another operation x1, loops' own time, shards(): shifted = lax.map(shifted_sector, sector_ids)  26.6 us
    another operation x1, loops' own time, shards(): direct = lax.map(direct_sector, sector_ids)  26 us
    dot_general x48, matrix products, apply_term(): jnp.einsum('iwa,nab->niwb', left[:, start:stop, :], source[:, shift], pre...  25 us
  transfers between devices with their start and end apart: 4, of which 2 were waited for; matrix products, arithmetic and copies ran while one was open for 1% of the time, Pallas kernels for 0%

commit v1 on v0

v1 whole, which is shorter than its diff:
```python
import functools
import math

import jax
import jax.numpy as jnp
from jax import lax
from jax.experimental import pallas as pl
from jax.experimental.pallas import tpu as pltpu
from jax.sharding import PartitionSpec as P

BF16, F32 = jnp.bfloat16, jnp.float32
VMEM_LIMIT = 50 << 20
CHUNKS = 2


def swap(x):
    return pltpu.roll(x, 64, 1)


def low_half():
    return lax.broadcasted_iota(jnp.int32, (1, 128), 1) < 64


def segments(pairs):
    low = pairs * 2 // 3 // 2
    return [(0, low), (low, pairs - low), (pairs - low, pairs)]


def spread(l_ref, g, rows, pairs):
    for c, (lo, hi) in enumerate(segments(pairs)):
        for t in range(lo, hi):
            g[pl.ds(c * 8 + t - lo, rows, stride=24), :] = l_ref[0, :, t * 128 : (t + 1) * 128].astype(F32)


def finish_mix(mx_ref, temp, o2, out_ref, pairs):
    lane = low_half()
    wide = mx_ref.shape[0]
    for u in range(16):
        y = jnp.dot(mx_ref[...], temp[u], preferred_element_type=F32)
        for t in range(2):
            o2[t, u * wide : (u + 1) * wide, :] = y[:, t * 128 : (t + 1) * 128]
    stride = wide // 4
    for e in range(2):
        for u in range(pairs // 2):
            first = 4 * u + e
            for t in range(2):
                x = o2[t, pl.ds(first, 64, stride=stride), :]
                y = o2[t, pl.ds(first + 2, 64, stride=stride), :]
                cols = slice(u * 128, (u + 1) * 128)
                out_ref[0, e, t * 128 : t * 128 + 64, cols] = jnp.where(lane, x, swap(y)).astype(BF16)
                out_ref[0, e, t * 128 + 64 : t * 128 + 128, cols] = jnp.where(lane, swap(x), y).astype(BF16)


def shifted_kernel(pairs, l_ref, s0_ref, s1_ref, s2_ref, mx_ref, out_ref, g, lq, bd, temp, o2):
    lane = low_half()

    @pl.when(pl.program_id(0) == 0)
    def _():
        g[...] = jnp.zeros_like(g)
        bd[...] = jnp.zeros_like(bd)

    spread(l_ref, g, 64, pairs)
    for pr in range(32):
        x = g[pl.ds(pr * 48, 24), :]
        y = g[pl.ds(pr * 48 + 24, 24), :]
        e = jnp.where(lane, x, swap(y))
        o = jnp.where(lane, swap(x), y)
        u, h = pr // 2, pr % 2
        for c in range(3):
            both = jnp.concatenate([e[c * 8 : c * 8 + 8], o[c * 8 : c * 8 + 8]], 0)
            lq[c, u * 16 : (u + 1) * 16, h * 128 : (h + 1) * 128] = both.astype(BF16)
    for c, s_ref in enumerate((s0_ref, s1_ref, s2_ref)):
        for t in range(2):
            x = s_ref[0, :, t * 128 : (t + 1) * 128].astype(F32)
            y = swap(x)
            z = jnp.zeros_like(x)
            for half, here, there in ((0, x, y), (1, y, x)):
                first = jnp.where(lane, here, z).astype(BF16)
                second = jnp.where(lane, z, there).astype(BF16)
                for b in range(4):
                    cols = slice((b // 2) * 128, (b // 2) * 128 + 128)
                    bd[c * 4 + 2 * t + half, b * 64 : b * 64 + 64, cols] = first if b % 2 == 0 else second
    for c in range(3):
        for p in range(4):
            y = jnp.dot(lq[c], bd[c * 4 + p], preferred_element_type=F32).astype(BF16)
            temp[:, p * 48 + c * 16 : p * 48 + c * 16 + 16, :] = y.reshape(16, 16, 256)
    finish_mix(mx_ref, temp, o2, out_ref, pairs)


def direct_kernel(pairs, rows, count, *refs):
    l_ref, sources, (mx_ref, out_ref, g, lq, ex, temp, o2) = refs[0], refs[1 : 1 + 3 * count], refs[1 + 3 * count :]
    lane = low_half()

    @pl.when(pl.program_id(0) == 0)
    def _():
        g[...] = jnp.zeros_like(g)
        ex[...] = jnp.zeros_like(ex)

    spread(l_ref, g, rows, pairs)
    for i in range(rows):
        for c in range(3):
            x = g[i * 24 + c * 8 : i * 24 + c * 8 + 8, :]
            lq[c, i * 16 : (i + 1) * 16, :] = jnp.concatenate([x, swap(x)], 0).astype(BF16)
    quads = 16 // rows
    for c in range(3):
        parts = [(r, m) for r in sources[c * count : (c + 1) * count] for m in range(r.shape[0])]
        for mg in range(quads):
            for h in range(2):
                (ra, ma), (rb, mb) = parts[4 * mg + 2 * h], parts[4 * mg + 2 * h + 1]
                for t in range(2):
                    x = ra[ma, 0, :, t * 128 : (t + 1) * 128].astype(F32)
                    y = rb[mb, 0, :, t * 128 : (t + 1) * 128].astype(F32)
                    cols = slice(h * 128, (h + 1) * 128)
                    ex[(c * 4 + 2 * t) * quads + mg, 0:64, cols] = jnp.where(lane, x, swap(y)).astype(BF16)
                    ex[(c * 4 + 2 * t + 1) * quads + mg, 0:64, cols] = jnp.where(lane, swap(x), y).astype(BF16)
        for p in range(4):
            for mg in range(quads):
                y = jnp.dot(lq[c], ex[(c * 4 + p) * quads + mg], preferred_element_type=F32).astype(BF16)
                temp[mg * rows : (mg + 1) * rows, p * 48 + c * 16 : p * 48 + c * 16 + 16, :] = y.reshape(rows, 16, 256)
    finish_mix(mx_ref, temp, o2, out_ref, pairs)


def close_kernel(pairs, count, offs_ref, a_ref, b_ref, *refs):
    pieces, (d0_ref, d1_ref, d2_ref, d3_ref, sh_ref, rs, res, fin) = refs[:count], refs[count:]
    lane = low_half()
    for k, piece in enumerate(pieces):
        size = piece.shape[1]
        for t in range(pairs):
            at = pl.multiple_of(offs_ref[k] + t * 64, size)
            rs[pl.ds(at, size), :] = piece[0, :, t * 128 : (t + 1) * 128]
    for term, ref in enumerate((a_ref, b_ref)):
        even = jnp.dot(ref[0, 0], rs[...], preferred_element_type=F32)
        odd = jnp.dot(ref[0, 1], rs[...], preferred_element_type=F32)
        res[...] = even + swap(odd)
        for t in range(2):
            x = res[pl.ds(2 * t, 64, stride=4), :]
            y = res[pl.ds(2 * t + 1, 64, stride=4), :]
            z = jnp.where(lane, x, swap(y))
            cols = slice(t * 128, (t + 1) * 128)
            if term == 0:
                for k, d_ref in enumerate((d0_ref, d1_ref, d2_ref, d3_ref)):
                    d_ref[0, :, cols] = z[k * 16 : (k + 1) * 16].astype(BF16)
            else:
                for k in range(4):
                    fin[t, pl.ds(k, 16, stride=4), :] = z[k * 16 : (k + 1) * 16]
                sh_ref[0, :, cols] = fin[t]


def combine_kernel(count, base, ints_ref, phase_ref, sh_ref, *refs):
    pieces, out_ref, rows = refs[:count], refs[-2], refs[-1]
    for k, piece in enumerate(pieces):
        size = piece.shape[1]
        rows[pl.ds(pl.multiple_of(ints_ref[k], size), size), :] = piece[0].astype(F32)
    used = ints_ref[count + base + pl.program_id(0)]
    i = lax.broadcasted_iota(jnp.int32, (64, 256), 0)
    k = lax.broadcasted_iota(jnp.int32, (64, 256), 1) % 64
    mask = ((i < used) & (k < used)).astype(F32)
    shifted = sh_ref[0]
    out_ref[0, 0, 0] = (mask * (rows[...] + phase_ref[0] * shifted)).astype(BF16)
    out_ref[0, 1, 0] = (-mask * phase_ref[1] * shifted).astype(BF16)


def params():
    return pltpu.CompilerParams(vmem_limit_bytes=VMEM_LIMIT)


def cost(flops, moved):
    return pl.CostEstimate(flops=int(flops), bytes_accessed=int(moved), transcendentals=0)


def regroup_mpo(mpo):
    width, phys = mpo.shape[:2]
    parts = []
    for lo, hi in segments(width // 2):
        part = mpo[2 * lo : 2 * hi].reshape(hi - lo, 2, phys, width, phys)
        parts.append(jnp.pad(part, ((0, 8 - (hi - lo)), (0, 0), (0, 0), (0, 0), (0, 0))))
    x = jnp.stack(parts).transpose(5, 4, 3, 0, 2, 1)
    return x.reshape(phys * width, phys * 48)


def mix_scratch(wide, pairs):
    return [pltpu.VMEM((16, 192, 256), BF16), pltpu.VMEM((2, 16 * wide, 128), F32)]


def mix_shifted(left, source, mx):
    sectors, rows, lanes = left.shape
    pairs, wide = lanes // 128, mx.shape[0]
    window = [pl.BlockSpec((1, 64, 256), lambda s, c=c: (s + c, 0, 0)) for c in range(3)]
    return pl.pallas_call(
        functools.partial(shifted_kernel, pairs),
        grid=(sectors,),
        in_specs=[pl.BlockSpec((1, rows, lanes), lambda s: (s, 0, 0))] + window + [pl.BlockSpec(mx.shape, lambda s: (0, 0))],
        out_specs=pl.BlockSpec((1, 2, 256, lanes // 2), lambda s: (s, 0, 0, 0)),
        out_shape=jax.ShapeDtypeStruct((sectors, 2, 256, lanes // 2), BF16),
        scratch_shapes=[pltpu.VMEM((64 * 24, 128), F32), pltpu.VMEM((3, 256, 256), BF16), pltpu.VMEM((12, 256, 256), BF16)]
        + mix_scratch(wide, pairs),
        compiler_params=params(),
        cost_estimate=cost(sectors * 1.2e9, sectors * 1.8e6),
        name="mix_shifted",
    )(left, source, source, source, mx)


def mix_direct(left, sources, mx):
    sectors, rows, lanes = left.shape
    pairs, wide = lanes // 128, mx.shape[0]
    window = [
        pl.BlockSpec((src.shape[0], 1, 64, 256), lambda s, c=c: (0, s + c, 0, 0)) for c in range(3) for src in sources
    ]
    return pl.pallas_call(
        functools.partial(direct_kernel, pairs, rows, len(sources)),
        grid=(sectors,),
        in_specs=[pl.BlockSpec((1, rows, lanes), lambda s: (s, 0, 0))] + window + [pl.BlockSpec(mx.shape, lambda s: (0, 0))],
        out_specs=pl.BlockSpec((1, 2, 256, lanes // 2), lambda s: (s, 0, 0, 0)),
        out_shape=jax.ShapeDtypeStruct((sectors, 2, 256, lanes // 2), BF16),
        scratch_shapes=[
            pltpu.VMEM((rows * 24, 128), F32),
            pltpu.VMEM((3, rows * 16, 128), BF16),
            pltpu.VMEM((12 * (16 // rows), 128, 256), BF16),
        ]
        + mix_scratch(wide, pairs),
        compiler_params=params(),
        cost_estimate=cost(sectors * 1.2e9, sectors * 1.8e6),
        name="mix_direct",
    )(left, *(list(sources) * 3), mx)


def close_terms(direct, shifted, pieces, offs, base):
    count, lanes = pieces[0].shape[0], pieces[0].shape[2]
    mixed = pl.BlockSpec((1, 2, 256, lanes // 2), lambda s: (s + base, 0, 0, 0))
    return pl.pallas_call(
        functools.partial(close_kernel, lanes // 128, len(pieces)),
        grid=(count,),
        in_specs=[pl.BlockSpec(memory_space=pltpu.SMEM), mixed, mixed]
        + [pl.BlockSpec((1,) + p.shape[1:], lambda s: (s, 0, 0)) for p in pieces],
        out_specs=[pl.BlockSpec((1, 16, 256), lambda s: (s, 0, 0))] * 4 + [pl.BlockSpec((1, 64, 256), lambda s: (s, 0, 0))],
        out_shape=[jax.ShapeDtypeStruct((count, 16, 256), BF16)] * 4 + [jax.ShapeDtypeStruct((count, 64, 256), F32)],
        scratch_shapes=[pltpu.VMEM((lanes // 2, 128), BF16), pltpu.VMEM((256, 128), F32), pltpu.VMEM((2, 64, 128), F32)],
        compiler_params=params(),
        cost_estimate=cost(count * 0.6e9, count * 3.3e6),
        name="close_terms",
    )(offs, direct, shifted, *pieces)


def combine(ints, phase, shifted, pieces, base, sectors, out):
    count = shifted.shape[0]
    specs = [pl.BlockSpec(memory_space=pltpu.SMEM), pl.BlockSpec(memory_space=pltpu.SMEM)]
    specs += [pl.BlockSpec((1,) + p.shape[1:], lambda s: (s, 0, 0)) for p in (shifted, *pieces)]
    args, alias = [ints, phase, shifted, *pieces], {}
    if out is not None:
        alias = {len(args): 0}
        args.append(out)
        specs.append(pl.BlockSpec(memory_space=pl.ANY))
    return pl.pallas_call(
        functools.partial(combine_kernel, len(pieces), base),
        grid=(count,),
        in_specs=specs,
        out_specs=pl.BlockSpec((1, 2, 1, 64, 256), lambda s: (0, 0, s + base, 0, 0)),
        out_shape=jax.ShapeDtypeStruct((1, 2, sectors, 64, 256), BF16),
        scratch_shapes=[pltpu.VMEM((64, 256), F32)],
        input_output_aliases=alias,
        compiler_params=params(),
        cost_estimate=cost(count * 1e5, count * 2e5),
        name="combine",
    )(*args)


def shards(left_env, right_env, left_mixed, excitation, ground, mpo, momentum, block_dims):
    sectors = excitation.shape[1]
    groups = lax.axis_size("mom")
    mine = lax.axis_index("mom")
    rows = left_env.shape[1]
    devices = lax.axis_size("sec")
    up = [(i, i + 1) for i in range(devices - 1)]
    down = [(i + 1, i) for i in range(devices - 1)]
    partner = [[(i, i ^ k) for i in range(groups)] for k in range(4)]
    step = sectors // CHUNKS

    stacked = jnp.stack([excitation[0], ground])
    before = lax.ppermute(stacked[:, sectors - 1 :], "sec", up)
    after = lax.ppermute(stacked[:, :1], "sec", down)
    padded = jnp.concatenate([before, stacked, after], axis=1)
    own = padded[:1]
    if groups == 4:
        sources = [own] + [lax.ppermute(own, "mom", partner[k]) for k in (1, 2, 3)]
    else:
        sources = [lax.all_gather(own[0], "mom")]
    rights = []
    if groups == 4:
        for c in range(CHUNKS):
            part = right_env[c * step : (c + 1) * step]
            rights.append([part] + [lax.ppermute(part, "mom", partner[k]) for k in (1, 2, 3)])
        offs = jnp.stack([mine ^ k for k in range(4)]).astype(jnp.int32) * rows
    else:
        full = lax.all_gather(right_env, "mom", axis=1, tiled=True)
        rights = [[full[c * step : (c + 1) * step]] for c in range(CHUNKS)]
        offs = jnp.zeros((1,), jnp.int32)

    mx = regroup_mpo(mpo)
    phase = 2.0 * math.pi * momentum[0].astype(F32) / groups
    waves = jnp.stack([jnp.cos(phase), jnp.sin(phase)])
    ints = jnp.concatenate([offs, block_dims])
    shifted = mix_shifted(left_mixed[0], padded[1], mx)
    direct = mix_direct(left_env, sources, mx)
    out = None
    for c in range(CHUNKS):
        *parts, held = close_terms(direct, shifted, rights[c], offs, c * step)
        if groups == 4:
            parts = [parts[0]] + [lax.ppermute(parts[k], "mom", partner[k]) for k in (1, 2, 3)]
        else:
            whole = jnp.stack(parts, 1).reshape(step, 4, groups // 4, rows, 256)
            whole = whole.transpose(0, 2, 1, 3, 4).reshape(step, groups, rows, 256)
            parts = [lax.all_to_all(whole, "mom", 1, 2, tiled=True).reshape(step, 64, 256)]
        out = combine(ints, waves, held, parts, c * step, sectors, out)
    return out


def solution(mesh):
    return jax.shard_map(
        shards,
        mesh=mesh,
        in_specs=(
            P("sec", "mom", None),
            P("sec", "mom", None),
            P("mom", "sec", None, None),
            P("mom", "sec", None, None),
            P("sec", None, None),
            P(),
            P("mom"),
            P("sec"),
        ),
        out_specs=P("mom", None, "sec", None, None),
        check_vma=False,
    )
```

time: 643 us -> 102 us (0.16)
  matrix products: 291 us -> 0 us
  local copies, waits for them, and re-layouts: 191 us -> 5.08 us
  waiting for transfers between devices: 80.1 us -> 23.9 us
  loops' own time: 52.6 us -> 0 us
  Pallas kernels: 0 us -> 44.1 us
  starting transfers between devices: 4.37 us -> 24.4 us
  between operations: 14.3 us -> 0.92 us
    dot_general x112 -> x0, matrix products: 291 us -> none  [the longest x48 220 us: apply_term(): jnp.einsum('niwpj,wpvq->nviqj', temp, mpo[start:stop], preferred_element_...]
    another operation x66 -> x1, local copies, waits for them, and re-layouts: 119 us -> 0.07 us  [regroup_mpo(): x = jnp.stack(parts).transpose(5, 4, 3, 0, 2, 1)]
    all_gather x2 -> x0, waiting for transfers between devices: 78.7 us -> none  [the longest x1 43.7 us: shards(): right_full = lax.all_gather(right_env, 'mom', axis=1, tiled=True)]
    another operation x2 -> x0, loops' own time: 52.6 us -> none  [the longest x1 26.6 us: shards(): shifted = lax.map(shifted_sector, sector_ids)]
    pallas_call x0 -> x6, Pallas kernels: none -> 44.1 us  [the longest x2 14.3 us: close_terms(): pl.pallas_call(functools.partial(close_kernel, lanes // 128, len(pieces))...]
    dynamic_slice x40 -> x0, local copies, waits for them, and re-layouts: 36.6 us -> none  [the longest x16 11.3 us: shards(): shifted = lax.map(shifted_sector, sector_ids)]
    ppermute x2 -> x17, waiting for transfers between devices: 0.01 us -> 23.9 us  [the longest x6 16.8 us: shards(): lax.ppermute(part, 'mom', partner[k])]
    ppermute x2 -> x17, starting transfers between devices: 4.33 us -> 24.4 us  [the longest x6 9.45 us: shards(): lax.ppermute(part, 'mom', partner[k])]
  transfers between devices with their start and end apart: 4 -> 17, of which waited for: 2 -> 4; matrix products, arithmetic and copies ran while one was open for 1% -> 5% of each run, Pallas kernels for 0% -> 42%
where the time goes in v1:
time: 102 us; the launch traced here: 101 us
  Pallas kernels  44.1 us (43%)
  starting transfers between devices  24.4 us (24%)
  waiting for transfers between devices  23.9 us (23%)
  local copies, waits for them, and re-layouts  5.08 us (5%)
  other arithmetic  2.96 us (3%)
    ppermute x6, waiting for transfers between devices, shards(): lax.ppermute(part, 'mom', partner[k])  16.8 us
    pallas_call x2, Pallas kernels, close_terms(): pl.pallas_call(functools.partial(close_kernel, lanes // 128, len(pieces))...  14.3 us
    pallas_call x1, Pallas kernels, mix_shifted(): pl.pallas_call(functools.partial(shifted_kernel, pairs), grid=(sectors,),...  13.1 us
    pallas_call x1, Pallas kernels, mix_direct(): pl.pallas_call(functools.partial(direct_kernel, pairs, rows, len(sources)...  12.8 us
    ppermute x6, starting transfers between devices, shards(): lax.ppermute(part, 'mom', partner[k])  9.45 us
    ppermute x6, starting transfers between devices, shards(): lax.ppermute(parts[k], 'mom', partner[k])  7.11 us
    pallas_call x2, Pallas kernels, combine(): pl.pallas_call(functools.partial(combine_kernel, len(pieces), base), grid...  3.92 us
    ppermute x3, waiting for transfers between devices, shards(): sources = [own] + [lax.ppermute(own, 'mom', partner[k]) for k in (1, 2, 3)]  3.81 us
  transfers between devices with their start and end apart: 17, of which 4 were waited for; matrix products, arithmetic and copies ran while one was open for 5% of the time, Pallas kernels for 42%

profile of v1, /device:TPU:0, one launch (start us, length us, event | category | flops | bytes accessed | tf_op | source)
XLA Modules:
  0.0 101.4 jit_solution(11116878583406577581)
XLA Ops:
  0.0 0.8 pad_maximum_fusion.2
  0.8 1.3 %collective-permute-start.1 = (bf16[2,1,64,256]{3,2,1,0:T(8,128)(2,1)S(1)}, bf16[2,1,64,256]{3,2,1,0:T(8,128)(2,1)S(1)}, u32[]{:S(2)}, u32[]{:S(2)}) collective-permute-start(bf16[2,1,64,256]{3,2,1,0:T(8,128)(2,1)S(1)} %get-tuple-element.30), channel_id=1, source_target_pairs={{1,0},{2,1},{3,2},{4,3},{5,4},{6,5},{7,6},{9,8},{10,9},{11,10},{12... | collective-permute-start | bytes 196616 | tf_op jit(solution)/shard_map/ppermute | solution.py:280
  2.1 3.0 %collective-permute-start = (bf16[2,1,64,256]{3,2,1,0:T(8,128)(2,1)S(1)}, bf16[2,1,64,256]{3,2,1,0:T(8,128)(2,1)S(1)}, u32[]{:S(2)}, u32[]{:S(2)}) collective-permute-start(bf16[2,1,64,256]{3,2,1,0:T(8,128)(2,1)S(1)} %get-tuple-element.29), channel_id=1, source_target_pairs={{0,1},{1,2},{2,3},{3,4},{4,5},{5,6},{6,7},{8,9},{9,10},{10,11},{11... | collective-permute-start | bytes 196616 | tf_op jit(solution)/shard_map/ppermute | solution.py:279
  5.2 1.1 %fusion = (bf16[4,16,2816]{2,1,0:T(8,128)(2,1)S(1)}, bf16[4,16,2816]{2,1,0:T(8,128)(2,1)S(1)}) fusion(bf16[8,16,2816]{2,1,0:T(8,128)(2,1)} %param.9), kind=kLoop, calls=%fused_computation.10 | loop fusion | bytes 1441792 | tf_op jit(solution)/shard_map/slice | solution.py:290
  6.3 3.0 %collective-permute-start.5 = (bf16[4,16,2816]{2,1,0:T(8,128)(2,1)S(1)}, bf16[4,16,2816]{2,1,0:T(8,128)(2,1)S(1)}, u32[]{:S(2)}, u32[]{:S(2)}) collective-permute-start(bf16[4,16,2816]{2,1,0:T(8,128)(2,1)S(1)} %get-tuple-element.26.refs_0_), channel_id=1, source_target_pairs={{0,8},{8,0},{16,24},{24,16},{1,9},{9,1},{17,25},{25,17},{2,10},{10... | collective-permute-start | bytes 1081352 | tf_op jit(solution)/shard_map/ppermute | solution.py:291
  9.3 0.1 collective-permute-start.11
  10.2 0.9 fusion.1
  11.1 0.9 slice.31
  12.0 0.1 pad_bitcast_fusion
  12.0 0.1 maximum_bitcast_fusion
  12.2 0.2 reshape.20
  12.3 0.1 copy.16.refs_13_.mx_ref
  12.4 0.1 add_multiply_fusion.offs_ref
  12.5 0.7 pad_add_fusion.ints_ref
  13.3 0.0 collective-permute-done.1
  13.3 0.0 collective-permute-done
  13.3 1.1 %pad_maximum_fusion = bf16[2,10,64,256]{3,2,1,0:T(8,128)(2,1)S(1)} fusion(bf16[2,1,64,256]{3,2,1,0:T(8,128)(2,1)S(1)} %collective-permute-done.1, bf16[1,8,64,256]{3,2,1,0:T(8,128)(2,1)} %bitcast.21, bf16[1,8,64,256]{3,2,1,0:T(8,128)(2,1)} %param.11, bf16[2,1,64,256]{3,2,1,0:T(8,128)(2,1)S(1)} %collective-permute-done), kind=kLoop, calls=%fused_computation | loop fusion | flops 983040 | bytes 1310720 | tf_op jit(solution)/shard_map/concatenate | solution.py:281
  14.4 2.0 %collective-permute-start.2 = (bf16[1,10,64,256]{3,2,1,0:T(8,128)(2,1)S(1)}, bf16[1,10,64,256]{3,2,1,0:T(8,128)(2,1)S(1)}, u32[]{:S(2)}, u32[]{:S(2)}) collective-permute-start(bf16[1,10,64,256]{3,2,1,0:T(8,128)(2,1)S(1)} %get-tuple-element.28.refs_1_.refs_5_.refs_9_), channel_id=1, source_target_pairs={{0,8},{8,0},{16,24},{24,16},{1,9},{9,1},{17,25},{25,17},{2,10},{10... | collective-permute-start | bytes 983048 | tf_op jit(solution)/shard_map/ppermute | solution.py:284
  16.5 1.5 %collective-permute-start.3 = (bf16[1,10,64,256]{3,2,1,0:T(8,128)(2,1)S(1)}, bf16[1,10,64,256]{3,2,1,0:T(8,128)(2,1)S(1)}, u32[]{:S(2)}, u32[]{:S(2)}) collective-permute-start(bf16[1,10,64,256]{3,2,1,0:T(8,128)(2,1)S(1)} %get-tuple-element.28.refs_1_.refs_5_.refs_9_), channel_id=1, source_target_pairs={{0,16},{8,24},{16,0},{24,8},{1,17},{9,25},{17,1},{25,9},{2,18},{10... | collective-permute-start | bytes 983048 | tf_op jit(solution)/shard_map/ppermute | solution.py:284
  18.0 0.0 collective-permute-start.4
  18.0 0.0 copy-start
  18.0 1.8 %copy-done = bf16[1,8,64,2816]{3,2,1,0:T(8,128)(2,1)S(1)} copy-done((bf16[1,8,64,2816]{3,2,1,0:T(8,128)(2,1)S(1)}, bf16[1,8,64,2816]{3,2,1,0:T(8,128)(2,1)}, u32[]{:S(2)}) %copy-start) | copy-done | bytes 2883608
  19.8 0.0 copy-start.1
  19.8 13.1 %mix_shifted.1.b_ref = bf16[8,2,256,1408]{3,2,1,0:T(8,128)(2,1)} custom-call(bf16[8,64,2816]{2,1,0:T(8,128)(2,1)S(1)} %bitcast.19, bf16[10,64,256]{2,1,0:T(8,128)(2,1)S(1)} %get-tuple-element.27.s0_ref.s1_ref.s2_ref, bf16[10,64,256]{2,1,0:T(8,128)(2,1)S(1)} %get-tuple-element.27.s0_ref.s1_ref.s2_ref, ...), custom_call_target="tpu_custom_call" | custom-call | flops 9600000000 | bytes 14400000 | tf_op jit(solution)/shard_map/mix_shifted/pallas_call | solution.py:189
  33.0 0.0 collective-permute-done.11.refs_1_
  33.0 2.0 %collective-permute-start.6 = (bf16[4,16,2816]{2,1,0:T(8,128)(2,1)S(1)}, bf16[4,16,2816]{2,1,0:T(8,128)(2,1)S(1)}, u32[]{:S(2)}, u32[]{:S(2)}) collective-permute-start(bf16[4,16,2816]{2,1,0:T(8,128)(2,1)S(1)} %get-tuple-element.26.refs_0_), channel_id=1, source_target_pairs={{0,16},{8,24},{16,0},{24,8},{1,17},{9,25},{17,1},{25,9},{2,18},{10... | collective-permute-start | bytes 1081352 | tf_op jit(solution)/shard_map/ppermute | solution.py:291
  34.9 0.0 collective-permute-done.2.refs_2_.refs_6_.refs_10_
  34.9 1.4 %collective-permute-start.7 = (bf16[4,16,2816]{2,1,0:T(8,128)(2,1)S(1)}, bf16[4,16,2816]{2,1,0:T(8,128)(2,1)S(1)}, u32[]{:S(2)}, u32[]{:S(2)}) collective-permute-start(bf16[4,16,2816]{2,1,0:T(8,128)(2,1)S(1)} %get-tuple-element.26.refs_0_), channel_id=1, source_target_pairs={{0,24},{8,16},{16,8},{24,0},{1,25},{9,17},{17,9},{25,1},{2,26},{10... | collective-permute-start | bytes 1081352 | tf_op jit(solution)/shard_map/ppermute | solution.py:291
  36.4 0.0 collective-permute-done.3.refs_3_.refs_7_.refs_11_
  36.4 1.5 %collective-permute-start.12 = (bf16[4,16,2816]{2,1,0:T(8,128)(2,1)S(1)}, bf16[4,16,2816]{2,1,0:T(8,128)(2,1)S(1)}, u32[]{:S(2)}, u32[]{:S(2)}) collective-permute-start(bf16[4,16,2816]{2,1,0:T(8,128)(2,1)S(1)} %get-tuple-element.25.refs_0_), channel_id=1, source_target_pairs={{0,16},{8,24},{16,0},{24,8},{1,17},{9,25},{17,1},{25,9},{2,18},{10... | collective-permute-start | bytes 1081352 | tf_op jit(solution)/shard_map/ppermute | solution.py:291
  37.9 3.8 %collective-permute-done.4.refs_4_.refs_8_.refs_12_ = bf16[1,10,64,256]{3,2,1,0:T(8,128)(2,1)S(1)} collective-permute-done((bf16[1,10,64,256]{3,2,1,0:T(8,128)(2,1)S(1)}, bf16[1,10,64,256]{3,2,1,0:T(8,128)(2,1)S(1)}, u32[]{:S(2)}, u32[]{:S(2)}) %collective-permute-start.4) | collective-permute-done | bytes 327712 | tf_op jit(solution)/shard_map/ppermute | solution.py:284
  41.7 1.4 %collective-permute-start.13 = (bf16[4,16,2816]{2,1,0:T(8,128)(2,1)S(1)}, bf16[4,16,2816]{2,1,0:T(8,128)(2,1)S(1)}, u32[]{:S(2)}, u32[]{:S(2)}) collective-permute-start(bf16[4,16,2816]{2,1,0:T(8,128)(2,1)S(1)} %get-tuple-element.25.refs_0_), channel_id=1, source_target_pairs={{0,24},{8,16},{16,8},{24,0},{1,25},{9,17},{17,9},{25,1},{2,26},{10... | collective-permute-start | bytes 1081352 | tf_op jit(solution)/shard_map/ppermute | solution.py:291
  43.1 0.0 copy-done.1
  43.1 12.8 %mix_direct.1.a_ref = bf16[8,2,256,1408]{3,2,1,0:T(8,128)(2,1)} custom-call(bf16[8,16,2816]{2,1,0:T(8,128)(2,1)S(1)} %copy-done.1, bf16[1,10,64,256]{3,2,1,0:T(8,128)(2,1)S(1)} %get-tuple-element.28.refs_1_.refs_5_.refs_9_, bf16[1,10,64,256]{3,2,1,0:T(8,128)(2,1)S(1)} %collective-permute-done.2.refs_2_.refs_6_.refs_10_, ...), custom_call_target="tpu_custom_call" | custom-call | flops 9600000000 | bytes 14400000 | tf_op jit(solution)/shard_map/mix_direct/pallas_call | solution.py:209
  55.9 16.8 %collective-permute-done.12.refs_2_ = bf16[4,16,2816]{2,1,0:T(8,128)(2,1)S(1)} collective-permute-done((bf16[4,16,2816]{2,1,0:T(8,128)(2,1)S(1)}, bf16[4,16,2816]{2,1,0:T(8,128)(2,1)S(1)}, u32[]{:S(2)}, u32[]{:S(2)}) %collective-permute-start.12) | collective-permute-done | bytes 360480 | tf_op jit(solution)/shard_map/ppermute | solution.py:291
  72.7 0.0 collective-permute-done.13.refs_3_
  72.7 7.1 %close_terms.3 = (bf16[4,16,256]{2,1,0:T(8,128)(2,1)S(1)}, bf16[4,16,256]{2,1,0:T(8,128)(2,1)S(1)}, bf16[4,16,256]{2,1,0:T(8,128)(2,1)S(1)}, bf16[4,16,256]{2,1,0:T(8,128)(2,1)S(1)}, f32[4,64,256]{2,1,0:T(8,128)S(1)}) custom-call(s32[4]{0:T(128)S(1)} %add_multiply_fusion.offs_ref, bf16[8,2,256,1408]{3,2,1,0:T(8,128)(2,1)} %mix_direct.1.a_ref, ...), custom_call_target="tpu_custom_call" | custom-call | flops 2400000000 | bytes 13200000 | tf_op jit(solution)/shard_map/close_terms/pallas_call | solution.py:230
  79.9 1.6 %collective-permute-start.14 = (bf16[4,16,256]{2,1,0:T(8,128)(2,1)S(1)}, bf16[4,16,256]{2,1,0:T(8,128)(2,1)S(1)}, u32[]{:S(2)}, u32[]{:S(2)}) collective-permute-start(bf16[4,16,256]{2,1,0:T(8,128)(2,1)S(1)} %get-tuple-element.22), channel_id=1, source_target_pairs={{0,8},{8,0},{16,24},{24,16},{1,9},{9,1},{17,25},{25,17},{2,10},{10... | collective-permute-start | bytes 98312 | tf_op jit(solution)/shard_map/ppermute | solution.py:308
  81.4 0.0 collective-permute-done.5.refs_1_
  81.4 0.0 collective-permute-done.6.refs_2_
  81.4 0.0 collective-permute-done.7.refs_3_
  81.4 7.1 %close_terms.2 = (bf16[4,16,256]{2,1,0:T(8,128)(2,1)S(1)}, bf16[4,16,256]{2,1,0:T(8,128)(2,1)S(1)}, bf16[4,16,256]{2,1,0:T(8,128)(2,1)S(1)}, bf16[4,16,256]{2,1,0:T(8,128)(2,1)S(1)}, f32[4,64,256]{2,1,0:T(8,128)S(1)}) custom-call(s32[4]{0:T(128)S(1)} %add_multiply_fusion.offs_ref, bf16[8,2,256,1408]{3,2,1,0:T(8,128)(2,1)} %mix_direct.1.a_ref, ...), custom_call_target="tpu_custom_call" | custom-call | flops 2400000000 | bytes 13200000 | tf_op jit(solution)/shard_map/close_terms/pallas_call | solution.py:230
  88.6 0.6 collective-permute-start.8
  89.2 0.1 collective-permute-start.9
  89.2 2.9 %collective-permute-start.10 = (bf16[4,16,256]{2,1,0:T(8,128)(2,1)S(1)}, bf16[4,16,256]{2,1,0:T(8,128)(2,1)S(1)}, u32[]{:S(2)}, u32[]{:S(2)}) collective-permute-start(bf16[4,16,256]{2,1,0:T(8,128)(2,1)S(1)} %get-tuple-element.19), channel_id=1, source_target_pairs={{0,24},{8,16},{16,8},{24,0},{1,25},{9,17},{17,9},{25,1},{2,26},{10... | collective-permute-start | bytes 98312 | tf_op jit(solution)/shard_map/ppermute | solution.py:308
  92.1 0.5 collective-permute-start.15
  92.6 0.0 collective-permute-done.14.refs_1_
  92.6 1.5 %collective-permute-start.16 = (bf16[4,16,256]{2,1,0:T(8,128)(2,1)S(1)}, bf16[4,16,256]{2,1,0:T(8,128)(2,1)S(1)}, u32[]{:S(2)}, u32[]{:S(2)}) collective-permute-start(bf16[4,16,256]{2,1,0:T(8,128)(2,1)S(1)} %get-tuple-element.24), channel_id=1, source_target_pairs={{0,24},{8,16},{16,8},{24,0},{1,25},{9,17},{17,9},{25,1},{2,26},{10... | collective-permute-start | bytes 98312 | tf_op jit(solution)/shard_map/ppermute | solution.py:308
  94.1 0.1 pad_maximum_fusion.3.phase_ref
  94.2 1.8 %collective-permute-done.15.refs_2_ = bf16[4,16,256]{2,1,0:T(8,128)(2,1)S(1)} collective-permute-done((bf16[4,16,256]{2,1,0:T(8,128)(2,1)S(1)}, bf16[4,16,256]{2,1,0:T(8,128)(2,1)S(1)}, u32[]{:S(2)}, u32[]{:S(2)}) %collective-permute-start.15) | collective-permute-done | bytes 32800 | tf_op jit(solution)/shard_map/ppermute | solution.py:308
  96.1 1.4 %collective-permute-done.16.refs_3_ = bf16[4,16,256]{2,1,0:T(8,128)(2,1)S(1)} collective-permute-done((bf16[4,16,256]{2,1,0:T(8,128)(2,1)S(1)}, bf16[4,16,256]{2,1,0:T(8,128)(2,1)S(1)}, u32[]{:S(2)}, u32[]{:S(2)}) %collective-permute-start.16) | collective-permute-done | bytes 32800 | tf_op jit(solution)/shard_map/ppermute | solution.py:308
  97.5 1.9 %combine.2.refs_4_ = bf16[1,2,8,64,256]{4,3,2,1,0:T(8,128)(2,1)} custom-call(s32[12]{0:T(128)S(1)} %pad_add_fusion.ints_ref, f32[2]{0:T(128)S(1)} %pad_maximum_fusion.3.phase_ref, f32[4,64,256]{2,1,0:T(8,128)S(1)} %get-tuple-element.20.sh_ref, bf16[4,16,256]{2,1,0:T(8,128)(2,1)S(1)} %get-tuple-element.21.refs_0_, ...), custom_call_target="tpu_custom_call" | custom-call | flops 400000 | bytes 800000 | tf_op jit(solution)/shard_map/combine/pallas_call | solution.py:253
  99.4 0.0 collective-permute-done.8.refs_1_
  99.4 0.0 collective-permute-done.9.refs_2_
  99.4 0.0 collective-permute-done.10.refs_3_
  99.4 2.0 %combine.3 = bf16[1,2,8,64,256]{4,3,2,1,0:T(8,128)(2,1)} custom-call(s32[12]{0:T(128)S(1)} %pad_add_fusion.ints_ref, f32[2]{0:T(128)S(1)} %pad_maximum_fusion.3.phase_ref, f32[4,64,256]{2,1,0:T(8,128)S(1)} %get-tuple-element.15.sh_ref, bf16[4,16,256]{2,1,0:T(8,128)(2,1)S(1)} %get-tuple-element.16.refs_0_, ...), custom_call_target="tpu_custom_call", output_to_operand_aliasing={{}: (7, {})} | custom-call | flops 400000 | bytes 800000 | tf_op jit(solution)/shard_map/combine/pallas_call | solution.py:253
  (1 shorter events, 0.0 us)
Async XLA Ops:
  0.8 12.4 %collective-permute-start.1 = (bf16[2,1,64,256]{3,2,1,0:T(8,128)(2,1)S(1)}, bf16[2,1,64,256]{3,2,1,0:T(8,128)(2,1)S(1)}, u32[]{:S(2)}, u32[]{:S(2)}) collective-permute-start(bf16[2,1,64,256]{3,2,1,0:T(8,128)(2,1)S(1)} %get-tuple-element.30), channel_id=1, source_target_pairs={{1,0},{2,1},{3,2},{4,3},{5,4},{6,5},{7,6},{9,8},{10,9},{11,10},{12... | collective-permute-start | bytes 196616 | tf_op jit(solution)/shard_map/ppermute | solution.py:280
  2.1 11.1 %collective-permute-start = (bf16[2,1,64,256]{3,2,1,0:T(8,128)(2,1)S(1)}, bf16[2,1,64,256]{3,2,1,0:T(8,128)(2,1)S(1)}, u32[]{:S(2)}, u32[]{:S(2)}) collective-permute-start(bf16[2,1,64,256]{3,2,1,0:T(8,128)(2,1)S(1)} %get-tuple-element.29), channel_id=1, source_target_pairs={{0,1},{1,2},{2,3},{3,4},{4,5},{5,6},{6,7},{8,9},{9,10},{10,11},{11... | collective-permute-start | bytes 196616 | tf_op jit(solution)/shard_map/ppermute | solution.py:279
  6.3 75.1 %collective-permute-start.5 = (bf16[4,16,2816]{2,1,0:T(8,128)(2,1)S(1)}, bf16[4,16,2816]{2,1,0:T(8,128)(2,1)S(1)}, u32[]{:S(2)}, u32[]{:S(2)}) collective-permute-start(bf16[4,16,2816]{2,1,0:T(8,128)(2,1)S(1)} %get-tuple-element.26.refs_0_), channel_id=1, source_target_pairs={{0,8},{8,0},{16,24},{24,16},{1,9},{9,1},{17,25},{25,17},{2,10},{10... | collective-permute-start | bytes 1081352 | tf_op jit(solution)/shard_map/ppermute | solution.py:291
  9.3 23.6 %collective-permute-start.11 = (bf16[4,16,2816]{2,1,0:T(8,128)(2,1)S(1)}, bf16[4,16,2816]{2,1,0:T(8,128)(2,1)S(1)}, u32[]{:S(2)}, u32[]{:S(2)}) collective-permute-start(bf16[4,16,2816]{2,1,0:T(8,128)(2,1)S(1)} %get-tuple-element.25.refs_0_), channel_id=1, source_target_pairs={{0,8},{8,0},{16,24},{24,16},{1,9},{9,1},{17,25},{25,17},{2,10},{10... | collective-permute-start | bytes 1081352 | tf_op jit(solution)/shard_map/ppermute | solution.py:291
  14.4 20.5 %collective-permute-start.2 = (bf16[1,10,64,256]{3,2,1,0:T(8,128)(2,1)S(1)}, bf16[1,10,64,256]{3,2,1,0:T(8,128)(2,1)S(1)}, u32[]{:S(2)}, u32[]{:S(2)}) collective-permute-start(bf16[1,10,64,256]{3,2,1,0:T(8,128)(2,1)S(1)} %get-tuple-element.28.refs_1_.refs_5_.refs_9_), channel_id=1, source_target_pairs={{0,8},{8,0},{16,24},{24,16},{1,9},{9,1},{17,25},{25,17},{2,10},{10... | collective-permute-start | bytes 983048 | tf_op jit(solution)/shard_map/ppermute | solution.py:284
  16.5 19.9 %collective-permute-start.3 = (bf16[1,10,64,256]{3,2,1,0:T(8,128)(2,1)S(1)}, bf16[1,10,64,256]{3,2,1,0:T(8,128)(2,1)S(1)}, u32[]{:S(2)}, u32[]{:S(2)}) collective-permute-start(bf16[1,10,64,256]{3,2,1,0:T(8,128)(2,1)S(1)} %get-tuple-element.28.refs_1_.refs_5_.refs_9_), channel_id=1, source_target_pairs={{0,16},{8,24},{16,0},{24,8},{1,17},{9,25},{17,1},{25,9},{2,18},{10... | collective-permute-start | bytes 983048 | tf_op jit(solution)/shard_map/ppermute | solution.py:284
  18.0 23.7 %collective-permute-start.4 = (bf16[1,10,64,256]{3,2,1,0:T(8,128)(2,1)S(1)}, bf16[1,10,64,256]{3,2,1,0:T(8,128)(2,1)S(1)}, u32[]{:S(2)}, u32[]{:S(2)}) collective-permute-start(bf16[1,10,64,256]{3,2,1,0:T(8,128)(2,1)S(1)} %get-tuple-element.28.refs_1_.refs_5_.refs_9_), channel_id=1, source_target_pairs={{0,24},{8,16},{16,8},{24,0},{1,25},{9,17},{17,9},{25,1},{2,26},{10... | collective-permute-start | bytes 983048 | tf_op jit(solution)/shard_map/ppermute | solution.py:284
  18.0 1.8 %copy-start = (bf16[1,8,64,2816]{3,2,1,0:T(8,128)(2,1)S(1)}, bf16[1,8,64,2816]{3,2,1,0:T(8,128)(2,1)}, u32[]{:S(2)}) copy-start(bf16[1,8,64,2816]{3,2,1,0:T(8,128)(2,1)} %param.10) | copy-start | bytes 8650756
  19.8 23.3 %copy-start.1 = (bf16[8,16,2816]{2,1,0:T(8,128)(2,1)S(1)}, bf16[8,16,2816]{2,1,0:T(8,128)(2,1)}, u32[]{:S(2)}) copy-start(bf16[8,16,2816]{2,1,0:T(8,128)(2,1)} %refs_0_.1) | copy-start | bytes 2162692
  33.0 48.5 %collective-permute-start.6 = (bf16[4,16,2816]{2,1,0:T(8,128)(2,1)S(1)}, bf16[4,16,2816]{2,1,0:T(8,128)(2,1)S(1)}, u32[]{:S(2)}, u32[]{:S(2)}) collective-permute-start(bf16[4,16,2816]{2,1,0:T(8,128)(2,1)S(1)} %get-tuple-element.26.refs_0_), channel_id=1, source_target_pairs={{0,16},{8,24},{16,0},{24,8},{1,17},{9,25},{17,1},{25,9},{2,18},{10... | collective-permute-start | bytes 1081352 | tf_op jit(solution)/shard_map/ppermute | solution.py:291
  34.9 46.5 %collective-permute-start.7 = (bf16[4,16,2816]{2,1,0:T(8,128)(2,1)S(1)}, bf16[4,16,2816]{2,1,0:T(8,128)(2,1)S(1)}, u32[]{:S(2)}, u32[]{:S(2)}) collective-permute-start(bf16[4,16,2816]{2,1,0:T(8,128)(2,1)S(1)} %get-tuple-element.26.refs_0_), channel_id=1, source_target_pairs={{0,24},{8,16},{16,8},{24,0},{1,25},{9,17},{17,9},{25,1},{2,26},{10... | collective-permute-start | bytes 1081352 | tf_op jit(solution)/shard_map/ppermute | solution.py:291
  36.4 36.3 %collective-permute-start.12 = (bf16[4,16,2816]{2,1,0:T(8,128)(2,1)S(1)}, bf16[4,16,2816]{2,1,0:T(8,128)(2,1)S(1)}, u32[]{:S(2)}, u32[]{:S(2)}) collective-permute-start(bf16[4,16,2816]{2,1,0:T(8,128)(2,1)S(1)} %get-tuple-element.25.refs_0_), channel_id=1, source_target_pairs={{0,16},{8,24},{16,0},{24,8},{1,17},{9,25},{17,1},{25,9},{2,18},{10... | collective-permute-start | bytes 1081352 | tf_op jit(solution)/shard_map/ppermute | solution.py:291
  41.7 31.0 %collective-permute-start.13 = (bf16[4,16,2816]{2,1,0:T(8,128)(2,1)S(1)}, bf16[4,16,2816]{2,1,0:T(8,128)(2,1)S(1)}, u32[]{:S(2)}, u32[]{:S(2)}) collective-permute-start(bf16[4,16,2816]{2,1,0:T(8,128)(2,1)S(1)} %get-tuple-element.25.refs_0_), channel_id=1, source_target_pairs={{0,24},{8,16},{16,8},{24,0},{1,25},{9,17},{17,9},{25,1},{2,26},{10... | collective-permute-start | bytes 1081352 | tf_op jit(solution)/shard_map/ppermute | solution.py:291
  79.9 12.8 %collective-permute-start.14 = (bf16[4,16,256]{2,1,0:T(8,128)(2,1)S(1)}, bf16[4,16,256]{2,1,0:T(8,128)(2,1)S(1)}, u32[]{:S(2)}, u32[]{:S(2)}) collective-permute-start(bf16[4,16,256]{2,1,0:T(8,128)(2,1)S(1)} %get-tuple-element.22), channel_id=1, source_target_pairs={{0,8},{8,0},{16,24},{24,16},{1,9},{9,1},{17,25},{25,17},{2,10},{10... | collective-permute-start | bytes 98312 | tf_op jit(solution)/shard_map/ppermute | solution.py:308
  88.6 10.8 %collective-permute-start.8 = (bf16[4,16,256]{2,1,0:T(8,128)(2,1)S(1)}, bf16[4,16,256]{2,1,0:T(8,128)(2,1)S(1)}, u32[]{:S(2)}, u32[]{:S(2)}) collective-permute-start(bf16[4,16,256]{2,1,0:T(8,128)(2,1)S(1)} %get-tuple-element.17), channel_id=1, source_target_pairs={{0,8},{8,0},{16,24},{24,16},{1,9},{9,1},{17,25},{25,17},{2,10},{10... | collective-permute-start | bytes 98312 | tf_op jit(solution)/shard_map/ppermute | solution.py:308
  89.2 10.2 %collective-permute-start.9 = (bf16[4,16,256]{2,1,0:T(8,128)(2,1)S(1)}, bf16[4,16,256]{2,1,0:T(8,128)(2,1)S(1)}, u32[]{:S(2)}, u32[]{:S(2)}) collective-permute-start(bf16[4,16,256]{2,1,0:T(8,128)(2,1)S(1)} %get-tuple-element.18), channel_id=1, source_target_pairs={{0,16},{8,24},{16,0},{24,8},{1,17},{9,25},{17,1},{25,9},{2,18},{10... | collective-permute-start | bytes 98312 | tf_op jit(solution)/shard_map/ppermute | solution.py:308
  89.2 10.2 %collective-permute-start.10 = (bf16[4,16,256]{2,1,0:T(8,128)(2,1)S(1)}, bf16[4,16,256]{2,1,0:T(8,128)(2,1)S(1)}, u32[]{:S(2)}, u32[]{:S(2)}) collective-permute-start(bf16[4,16,256]{2,1,0:T(8,128)(2,1)S(1)} %get-tuple-element.19), channel_id=1, source_target_pairs={{0,24},{8,16},{16,8},{24,0},{1,25},{9,17},{17,9},{25,1},{2,26},{10... | collective-permute-start | bytes 98312 | tf_op jit(solution)/shard_map/ppermute | solution.py:308
  92.1 3.9 %collective-permute-start.15 = (bf16[4,16,256]{2,1,0:T(8,128)(2,1)S(1)}, bf16[4,16,256]{2,1,0:T(8,128)(2,1)S(1)}, u32[]{:S(2)}, u32[]{:S(2)}) collective-permute-start(bf16[4,16,256]{2,1,0:T(8,128)(2,1)S(1)} %get-tuple-element.23), channel_id=1, source_target_pairs={{0,16},{8,24},{16,0},{24,8},{1,17},{9,25},{17,1},{25,9},{2,18},{10... | collective-permute-start | bytes 98312 | tf_op jit(solution)/shard_map/ppermute | solution.py:308
  92.6 4.8 %collective-permute-start.16 = (bf16[4,16,256]{2,1,0:T(8,128)(2,1)S(1)}, bf16[4,16,256]{2,1,0:T(8,128)(2,1)S(1)}, u32[]{:S(2)}, u32[]{:S(2)}) collective-permute-start(bf16[4,16,256]{2,1,0:T(8,128)(2,1)S(1)} %get-tuple-element.24), channel_id=1, source_target_pairs={{0,24},{8,16},{16,8},{24,0},{1,25},{9,17},{17,9},{25,1},{2,26},{10... | collective-permute-start | bytes 98312 | tf_op jit(solution)/shard_map/ppermute | solution.py:308

commit v2 on v1

v2 whole, which is shorter than its diff:
```python
import functools
import math

import jax
import jax.numpy as jnp
from jax import lax
from jax.experimental import pallas as pl
from jax.experimental.pallas import tpu as pltpu
from jax.sharding import PartitionSpec as P

BF16, F32 = jnp.bfloat16, jnp.float32
VMEM_LIMIT = 24 << 20


def swap(x):
    return pltpu.roll(x, 64, 1)


def low_half():
    return lax.broadcasted_iota(jnp.int32, (1, 128), 1) < 64


def segments(pairs):
    low = pairs * 2 // 3 // 2
    return [(0, low), (low, pairs - low), (pairs - low, pairs)]


def spread(l_ref, g, rows, pairs):
    for c, (lo, hi) in enumerate(segments(pairs)):
        for t in range(lo, hi):
            g[pl.ds(c * 8 + t - lo, rows, stride=24), :] = l_ref[0, :, t * 128 : (t + 1) * 128].astype(F32)


def finish_mix(mx_ref, temp, o2, out_ref, pairs):
    lane = low_half()
    wide = mx_ref.shape[0]
    stride = wide // 4

    def contract(group):
        for u in range(4 * group, 4 * group + 4):
            y = jnp.dot(mx_ref[...], temp[u], preferred_element_type=F32)
            for t in range(2):
                o2[group][t, (u - 4 * group) * wide : (u - 4 * group + 1) * wide, :] = y[:, t * 128 : (t + 1) * 128]

    def regroup(group):
        for e in range(2):
            for u in range(pairs // 2):
                first = 4 * u + e
                for t in range(2):
                    x = o2[group][t, pl.ds(first, 16, stride=stride), :]
                    y = o2[group][t, pl.ds(first + 2, 16, stride=stride), :]
                    row = t * 128 + group * 16
                    cols = slice(u * 128, (u + 1) * 128)
                    out_ref[0, e, row : row + 16, cols] = jnp.where(lane, x, swap(y)).astype(BF16)
                    out_ref[0, e, row + 64 : row + 80, cols] = jnp.where(lane, swap(x), y).astype(BF16)

    for group in range(4):
        contract(group)
        if group:
            regroup(group - 1)
    regroup(3)


def regroup_mpo(mpo_ref, mx_ref, pairs):
    rows, width = mpo_ref.shape
    wide, cols = mx_ref.shape
    col = lax.broadcasted_iota(jnp.int32, (cols, 1), 0)
    p = (col >= 48).astype(jnp.int32) + (col >= 96).astype(jnp.int32) + (col >= 144).astype(jnp.int32)
    rest = col - 48 * p
    w = jnp.full((cols, 1), -1, jnp.int32)
    for c, (lo, hi) in enumerate(segments(pairs)):
        pair = rest % 8
        here = (rest // 16 == c) & (pair < hi - lo)
        w = jnp.where(here, 2 * (lo + pair) + (rest // 8) % 2, w)
    source = jnp.where(w < 0, -4 * 4, (w * 4 + p) * 4)
    row = lax.broadcasted_iota(jnp.int32, (1, rows), 1)
    total = jnp.zeros((wide, cols), F32)
    for q in range(4):
        pick = (row == source + q).astype(F32).astype(BF16)
        part = lax.dot_general(mpo_ref[...], pick, (((0,), (1,)), ((), ())), preferred_element_type=F32).astype(BF16)
        place = lax.broadcasted_iota(jnp.int32, (wide, width), 0) == lax.broadcasted_iota(jnp.int32, (wide, width), 1) + q * width
        total += jnp.dot(place.astype(F32).astype(BF16), part, preferred_element_type=F32)
    mx_ref[...] = total.astype(BF16)


def shifted_kernel(pairs, l_ref, s0_ref, s1_ref, s2_ref, before_ref, after_ref, mpo_ref, out_ref, mx_ref, g, lq, bd, temp, *o2):
    lane = low_half()
    step, last = pl.program_id(0), pl.num_programs(0) - 1

    @pl.when(pl.program_id(0) == 0)
    def _():
        g[...] = jnp.zeros_like(g)
        bd[...] = jnp.zeros_like(bd)
        regroup_mpo(mpo_ref, mx_ref, pairs)

    spread(l_ref, g, 64, pairs)
    for pr in range(32):
        x = g[pl.ds(pr * 48, 24), :]
        y = g[pl.ds(pr * 48 + 24, 24), :]
        e = jnp.where(lane, x, swap(y))
        o = jnp.where(lane, swap(x), y)
        u, h = pr // 2, pr % 2
        for c in range(3):
            both = jnp.concatenate([e[c * 8 : c * 8 + 8], o[c * 8 : c * 8 + 8]], 0)
            lq[c, u * 16 : (u + 1) * 16, h * 128 : (h + 1) * 128] = both.astype(BF16)
    for c, s_ref in enumerate((s0_ref, s1_ref, s2_ref)):
        for t in range(2):
            x = s_ref[0, :, t * 128 : (t + 1) * 128].astype(F32)
            if c == 0:
                x = jnp.where(step == 0, before_ref[0, 0, :, t * 128 : (t + 1) * 128].astype(F32), x)
            if c == 2:
                x = jnp.where(step == last, after_ref[0, 0, :, t * 128 : (t + 1) * 128].astype(F32), x)
            y = swap(x)
            z = jnp.zeros_like(x)
            for half, here, there in ((0, x, y), (1, y, x)):
                first = jnp.where(lane, here, z).astype(BF16)
                second = jnp.where(lane, z, there).astype(BF16)
                for b in range(4):
                    cols = slice((b // 2) * 128, (b // 2) * 128 + 128)
                    bd[c * 4 + 2 * t + half, b * 64 : b * 64 + 64, cols] = first if b % 2 == 0 else second
    for c in range(3):
        for p in range(4):
            y = jnp.dot(lq[c], bd[c * 4 + p], preferred_element_type=F32).astype(BF16)
            temp[:, p * 48 + c * 16 : p * 48 + c * 16 + 16, :] = y.reshape(16, 16, 256)
    finish_mix(mx_ref, temp, o2, out_ref, pairs)


def direct_kernel(pairs, rows, count, *refs):
    l_ref, sources, (mx_ref, out_ref, g, lq, ex, temp, *o2) = refs[0], refs[1 : 1 + 3 * count], refs[1 + 3 * count :]
    lane = low_half()

    @pl.when(pl.program_id(0) == 0)
    def _():
        g[...] = jnp.zeros_like(g)
        ex[...] = jnp.zeros_like(ex)

    spread(l_ref, g, rows, pairs)
    for i in range(rows):
        for c in range(3):
            x = g[i * 24 + c * 8 : i * 24 + c * 8 + 8, :]
            lq[c, i * 16 : (i + 1) * 16, :] = jnp.concatenate([x, swap(x)], 0).astype(BF16)
    quads = 16 // rows
    for c in range(3):
        parts = [(r, m) for r in sources[c * count : (c + 1) * count] for m in range(r.shape[0])]
        for mg in range(quads):
            for h in range(2):
                (ra, ma), (rb, mb) = parts[4 * mg + 2 * h], parts[4 * mg + 2 * h + 1]
                for t in range(2):
                    x = ra[ma, 0, :, t * 128 : (t + 1) * 128].astype(F32)
                    y = rb[mb, 0, :, t * 128 : (t + 1) * 128].astype(F32)
                    cols = slice(h * 128, (h + 1) * 128)
                    ex[(c * 4 + 2 * t) * quads + mg, 0:64, cols] = jnp.where(lane, x, swap(y)).astype(BF16)
                    ex[(c * 4 + 2 * t + 1) * quads + mg, 0:64, cols] = jnp.where(lane, swap(x), y).astype(BF16)
        for p in range(4):
            for mg in range(quads):
                y = jnp.dot(lq[c], ex[(c * 4 + p) * quads + mg], preferred_element_type=F32).astype(BF16)
                temp[mg * rows : (mg + 1) * rows, p * 48 + c * 16 : p * 48 + c * 16 + 16, :] = y.reshape(rows, 16, 256)
    finish_mix(mx_ref, temp, o2, out_ref, pairs)


def close_kernel(pairs, spans, direct, count, mixed_ref, *refs):
    pieces, outs, (rs, res, fin) = refs[:count], refs[count:-3], refs[-3:]
    lane = low_half()

    def sector(parts, s):
        for n, k, base in parts:
            size = pieces[n].shape[1]
            start = 0 if k is None else (lax.axis_index("mom") ^ k) * size
            for t in range(pairs):
                at = pl.multiple_of(start + t * 64, size)
                rs[pl.ds(at, size), :] = pieces[n][s - base, :, t * 128 : (t + 1) * 128]
        even = jnp.dot(mixed_ref[s, 0], rs[...], preferred_element_type=F32)
        odd = jnp.dot(mixed_ref[s, 1], rs[...], preferred_element_type=F32)
        res[...] = even + swap(odd)
        for t in range(2):
            x = res[pl.ds(2 * t, 64, stride=4), :]
            y = res[pl.ds(2 * t + 1, 64, stride=4), :]
            z = jnp.where(lane, x, swap(y))
            cols = slice(t * 128, (t + 1) * 128)
            if direct:
                for k, out_ref in enumerate(outs):
                    out_ref[s, :, cols] = z[k * 16 : (k + 1) * 16].astype(BF16)
            else:
                for k in range(4):
                    fin[t, pl.ds(k, 16, stride=4), :] = z[k * 16 : (k + 1) * 16]
                outs[0][s, :, cols] = fin[t]

    for lo, hi, parts in spans:
        pl.loop(lo, hi)(functools.partial(sector, parts))


def combine_kernel(dims_ref, turn_ref, shifted_ref, *refs):
    pieces, out_ref, rows = refs[:-2], refs[-2], refs[-1]
    phase = jnp.full((8, 256), turn_ref[0], F32)
    cos, sin = jnp.cos(phase)[:1], jnp.sin(phase)[:1]
    i = lax.broadcasted_iota(jnp.int32, (64, 256), 0)
    k = lax.broadcasted_iota(jnp.int32, (64, 256), 1) % 64
    for s in range(shifted_ref.shape[0]):
        shifted = shifted_ref[s]
        for n, piece in enumerate(pieces):
            size = piece.shape[1]
            start = 0 if len(pieces) == 1 else (lax.axis_index("mom") ^ n) * size
            rows[s, pl.ds(pl.multiple_of(start, size), size), :] = piece[s].astype(F32)
        mask = ((i < dims_ref[s]) & (k < dims_ref[s])).astype(F32)
        out_ref[0, 0, s] = (mask * (rows[s] + cos * shifted)).astype(BF16)
        out_ref[0, 1, s] = (-mask * sin * shifted).astype(BF16)


def params():
    return pltpu.CompilerParams(vmem_limit_bytes=VMEM_LIMIT)


def cost(flops, moved):
    return pl.CostEstimate(flops=int(flops), bytes_accessed=int(moved), transcendentals=0)


def mix_scratch(wide, pairs):
    return [pltpu.VMEM((16, 192, 256), BF16), *[pltpu.VMEM((2, 4 * wide, 128), F32)] * 4]


def mix_shifted(left, source, before, after, mpo):
    sectors, rows, lanes = left.shape
    width, phys = mpo.shape[:2]
    pairs, wide = lanes // 128, width * phys
    near = [
        pl.BlockSpec((1, 64, 256), lambda s, c=c: (jnp.clip(s + c - 1, 0, sectors - 1), 0, 0)) for c in range(3)
    ]
    edge = pl.BlockSpec((1, 1, 64, 256), lambda s: (1, 0, 0, 0))
    return pl.pallas_call(
        functools.partial(shifted_kernel, pairs),
        grid=(sectors,),
        in_specs=[pl.BlockSpec((1, rows, lanes), lambda s: (s, 0, 0))] + near + [edge, edge, pl.BlockSpec((wide * phys, width), lambda s: (0, 0))],
        out_specs=[
            pl.BlockSpec((1, 2, 256, lanes // 2), lambda s: (s, 0, 0, 0)),
            pl.BlockSpec((wide, 48 * phys), lambda s: (0, 0)),
        ],
        out_shape=[
            jax.ShapeDtypeStruct((sectors, 2, 256, lanes // 2), BF16),
            jax.ShapeDtypeStruct((wide, 48 * phys), BF16),
        ],
        scratch_shapes=[pltpu.VMEM((64 * 24, 128), F32), pltpu.VMEM((3, 256, 256), BF16), pltpu.VMEM((12, 256, 256), BF16)]
        + mix_scratch(wide, pairs),
        compiler_params=params(),
        cost_estimate=cost(sectors * 0.12e9, sectors * 0.18e6),
        name="mix_shifted",
    )(left, source, source, source, before, after, mpo.transpose(0, 1, 3, 2).reshape(wide * phys, width))


def mix_direct(left, sources, mx):
    sectors, rows, lanes = left.shape
    pairs, wide = lanes // 128, mx.shape[0]
    window = [
        pl.BlockSpec((src.shape[0], 1, 64, 256), lambda s, c=c: (0, s + c, 0, 0)) for c in range(3) for src in sources
    ]
    return pl.pallas_call(
        functools.partial(direct_kernel, pairs, rows, len(sources)),
        grid=(sectors,),
        in_specs=[pl.BlockSpec((1, rows, lanes), lambda s: (s, 0, 0))] + window + [pl.BlockSpec(mx.shape, lambda s: (0, 0))],
        out_specs=pl.BlockSpec((1, 2, 256, lanes // 2), lambda s: (s, 0, 0, 0)),
        out_shape=jax.ShapeDtypeStruct((sectors, 2, 256, lanes // 2), BF16),
        scratch_shapes=[
            pltpu.VMEM((rows * 24, 128), F32),
            pltpu.VMEM((3, rows * 16, 128), BF16),
            pltpu.VMEM((12 * (16 // rows), 128, 256), BF16),
        ]
        + mix_scratch(wide, pairs),
        compiler_params=params(),
        cost_estimate=cost(sectors * 1.2e9, sectors * 1.8e6),
        name="mix_direct",
    )(left, *(list(sources) * 3), mx)


def close(mixed, pieces, direct):
    lanes, sectors = pieces[0][0].shape[2], mixed.shape[0]
    cuts = sorted({0, sectors} | {lo for _, _, lo in pieces})
    spans = []
    for lo, hi in zip(cuts, cuts[1:]):
        parts = [(n, k, base) for n, (p, k, base) in enumerate(pieces) if base <= lo and hi <= base + p.shape[0]]
        spans.append((lo, hi, parts))
    rows, kind, count = (16, BF16, 4) if direct else (64, F32, 1)
    vmem = pl.BlockSpec(memory_space=pltpu.VMEM)
    return pl.pallas_call(
        functools.partial(close_kernel, lanes // 128, spans, direct, len(pieces)),
        in_specs=[vmem] * (1 + len(pieces)),
        out_specs=[vmem] * count,
        out_shape=[jax.ShapeDtypeStruct((sectors, rows, 256), kind)] * count,
        scratch_shapes=[pltpu.VMEM((lanes // 2, 128), BF16), pltpu.VMEM((256, 128), F32), pltpu.VMEM((2, 64, 128), F32)],
        compiler_params=params(),
        cost_estimate=cost(sectors * 0.3e9, sectors * 1.8e6),
        name="close_direct" if direct else "close_shifted",
    )(mixed, *[p for p, _, _ in pieces])


def combine(dims, turn, shifted, pieces):
    sectors = shifted.shape[0]
    vmem, smem = pl.BlockSpec(memory_space=pltpu.VMEM), pl.BlockSpec(memory_space=pltpu.SMEM)
    return pl.pallas_call(
        combine_kernel,
        in_specs=[smem, smem] + [vmem] * (1 + len(pieces)),
        out_specs=vmem,
        out_shape=jax.ShapeDtypeStruct((1, 2, sectors, 64, 256), BF16),
        scratch_shapes=[pltpu.VMEM((sectors, 64, 256), F32)],
        compiler_params=params(),
        cost_estimate=cost(sectors * 1e5, sectors * 2e5),
        name="combine",
    )(dims, turn, shifted, *pieces)


def shards(left_env, right_env, left_mixed, excitation, ground, mpo, momentum, block_dims):
    sectors = excitation.shape[1]
    groups = lax.axis_size("mom")
    rows = left_env.shape[1]
    devices = lax.axis_size("sec")
    up = [(i, i + 1) for i in range(devices - 1)]
    down = [(i + 1, i) for i in range(devices - 1)]
    partner = [[(i, i ^ k) for i in range(groups)] for k in range(4)]
    fast = groups == 4 and sectors % 2 == 0
    hop = [functools.partial(lax.ppermute, axis_name="mom", perm=p) for p in partner]
    stacked = jnp.stack([excitation[0], ground])
    before = lax.ppermute(stacked[:, sectors - 1 :], "sec", up)
    after = lax.ppermute(stacked[:, :1], "sec", down)
    own = jnp.concatenate([before[:1], excitation, after[:1]], axis=1)
    if fast:
        half = sectors // 2
        right1, right2 = hop[1](right_env), hop[2](right_env)
        sources = [own] + [hop[k](own) for k in (1, 2, 3)]
        low3, high3 = hop[2](right1[:half]), hop[1](right2[half:])
        pieces = [(right_env, 0, 0), (right1, 1, 0), (right2, 2, 0), (low3, 3, 0), (high3, 3, half)]
    else:
        sources = [lax.all_gather(own[0], "mom")]
        pieces = [(lax.all_gather(right_env, "mom", axis=1, tiled=True), None, 0)]
    turn = 2.0 * math.pi * momentum.astype(F32) / groups
    shifted, mx = mix_shifted(left_mixed[0], ground, before, after, mpo)
    direct = mix_direct(left_env, sources, mx)
    parts = close(direct, pieces, True)
    (held,) = close(shifted, pieces, False)
    if fast:
        parts = [parts[0]] + [hop[k](parts[k]) for k in (1, 2, 3)]
    else:
        whole = jnp.stack(parts, 1).reshape(sectors, 4, groups // 4, rows, 256)
        whole = whole.transpose(0, 2, 1, 3, 4).reshape(sectors, groups, rows, 256)
        parts = [lax.all_to_all(whole, "mom", 1, 2, tiled=True).reshape(sectors, 64, 256)]
    return combine(block_dims, turn, held, parts)


def solution(mesh):
    return jax.shard_map(
        shards,
        mesh=mesh,
        in_specs=(
            P("sec", "mom", None),
            P("sec", "mom", None),
            P("mom", "sec", None, None),
            P("mom", "sec", None, None),
            P("sec", None, None),
            P(),
            P("mom"),
            P("sec"),
        ),
        out_specs=P("mom", None, "sec", None, None),
        check_vma=False,
    )
```

time: 102 us -> 64.3 us (0.63)
  waiting for transfers between devices: 23.9 us -> 2.28 us
  starting transfers between devices: 24.4 us -> 16.7 us
  Pallas kernels: 44.1 us -> 37.5 us
  other arithmetic: 2.96 us -> 1.81 us
    ppermute x15 -> x10, waiting for transfers between devices: 23.9 us -> 1.42 us  [the longest x3 1.4 us: shards(): sources = [own] + [hop[k](own) for k in (1, 2, 3)]]
    ppermute x15 -> x10, starting transfers between devices: 20.1 us -> 12.3 us  [the longest x2 4.46 us: shards(): right1, right2 = (hop[1](right_env), hop[2](right_env))]
    pallas_call x4 -> x3, Pallas kernels: 18.2 us -> 13.1 us  [the longest x2 11.5 us: close(): pl.pallas_call(functools.partial(close_kernel, lanes // 128, spans, direc...]
    unnamed x4 -> x12, local copies, waits for them, and re-layouts: 1.82 us -> 4.8 us
    slice x3 -> x4, local copies, waits for them, and re-layouts: 2.9 us -> 0.06 us  [the longest x2 0.05 us: shards(): low3, high3 = (hop[2](right1[:half]), hop[1](right2[half:]))]
    pallas_call x1, Pallas kernels: 12.8 us -> 11.2 us  [mix_direct(): pl.pallas_call(functools.partial(direct_kernel, pairs, rows, len(sources)...]
  transfers between devices with their start and end apart: 17 -> 12, of which waited for: 4 -> 2; matrix products, arithmetic and copies ran while one was open for 5% -> 3% of each run, Pallas kernels for 42% -> 47%
where the time goes in v2:
time: 64.3 us; the launch traced here: 63.9 us
  Pallas kernels  37.5 us (58%)
  starting transfers between devices  16.7 us (26%)
  local copies, waits for them, and re-layouts  4.86 us (8%)
  waiting for transfers between devices  2.28 us (4%)
  other arithmetic  1.81 us (3%)
  between operations  0.82 us (1%)
    pallas_call x1, Pallas kernels, mix_shifted(): pl.pallas_call(functools.partial(shifted_kernel, pairs), grid=(sectors,),...  13.2 us
    pallas_call x2, Pallas kernels, close(): pl.pallas_call(functools.partial(close_kernel, lanes // 128, spans, direc...  11.5 us
    pallas_call x1, Pallas kernels, mix_direct(): pl.pallas_call(functools.partial(direct_kernel, pairs, rows, len(sources)...  11.2 us
    unnamed x12, local copies, waits for them, and re-layouts  4.8 us
    ppermute x2, starting transfers between devices, shards(): right1, right2 = (hop[1](right_env), hop[2](right_env))  4.46 us
    ppermute x3, starting transfers between devices, shards(): parts = [parts[0]] + [hop[k](parts[k]) for k in (1, 2, 3)]  3.55 us
    ppermute x3, starting transfers between devices, shards(): sources = [own] + [hop[k](own) for k in (1, 2, 3)]  3.55 us
    ppermute x1, starting transfers between devices, shards(): before = lax.ppermute(stacked[:, sectors - 1:], 'sec', up)  3.03 us
  transfers between devices with their start and end apart: 12, of which 2 were waited for; matrix products, arithmetic and copies ran while one was open for 3% of the time, Pallas kernels for 47%

profile of v2, /device:TPU:0, one launch (start us, length us, event | category | flops | bytes accessed | tf_op | source)
XLA Modules:
  0.0 63.9 jit_solution(15528302831509098453)
XLA Ops:
  0.0 3.0 %collective-permute-start.3 = (bf16[8,16,2816]{2,1,0:T(8,128)(2,1)}, bf16[8,16,2816]{2,1,0:T(8,128)(2,1)S(1)}, u32[]{:S(2)}, u32[]{:S(2)}) collective-permute-start(bf16[8,16,2816]{2,1,0:T(8,128)(2,1)} %refs_0_.5), channel_id=1, source_target_pairs={{0,16},{8,24},{16,0},{24,8},{1,17},{9,25},{17,1},{25,9},{2,18},{10... | collective-permute-start | bytes 2162696 | tf_op jit(solution)/shard_map/ppermute | solution.py:325
  3.0 1.5 %collective-permute-start.2 = (bf16[8,16,2816]{2,1,0:T(8,128)(2,1)}, bf16[8,16,2816]{2,1,0:T(8,128)(2,1)S(1)}, u32[]{:S(2)}, u32[]{:S(2)}) collective-permute-start(bf16[8,16,2816]{2,1,0:T(8,128)(2,1)} %refs_0_.5), channel_id=1, source_target_pairs={{0,8},{8,0},{16,24},{24,16},{1,9},{9,1},{17,25},{25,17},{2,10},{10... | collective-permute-start | bytes 2162696 | tf_op jit(solution)/shard_map/ppermute | solution.py:325
  4.5 0.8 %pad_maximum_fusion.1 = (bf16[2,1,64,256]{3,2,1,0:T(8,128)(2,1)S(1)}, bf16[2,1,64,256]{3,2,1,0:T(8,128)(2,1)S(1)}) fusion(bf16[1,8,64,256]{3,2,1,0:T(8,128)(2,1)} %bitcast.5, bf16[1,8,64,256]{3,2,1,0:T(8,128)(2,1)} %param.11), kind=kLoop, calls=%fused_computation.1 | loop fusion | flops 65536 | bytes 655360 | tf_op jit(solution)/shard_map/stack | solution.py:319
  5.3 1.3 %collective-permute-start.1 = (bf16[2,1,64,256]{3,2,1,0:T(8,128)(2,1)S(1)}, bf16[2,1,64,256]{3,2,1,0:T(8,128)(2,1)S(1)}, u32[]{:S(2)}, u32[]{:S(2)}) collective-permute-start(bf16[2,1,64,256]{3,2,1,0:T(8,128)(2,1)S(1)} %get-tuple-element.17), channel_id=1, source_target_pairs={{1,0},{2,1},{3,2},{4,3},{5,4},{6,5},{7,6},{9,8},{10,9},{11,10},{12... | collective-permute-start | bytes 196616 | tf_op jit(solution)/shard_map/ppermute | solution.py:321
  6.6 3.0 %collective-permute-start = (bf16[2,1,64,256]{3,2,1,0:T(8,128)(2,1)S(1)}, bf16[2,1,64,256]{3,2,1,0:T(8,128)(2,1)S(1)}, u32[]{:S(2)}, u32[]{:S(2)}) collective-permute-start(bf16[2,1,64,256]{3,2,1,0:T(8,128)(2,1)S(1)} %get-tuple-element.18), channel_id=1, source_target_pairs={{0,1},{1,2},{2,3},{3,4},{4,5},{5,6},{6,7},{8,9},{9,10},{10,11},{11... | collective-permute-start | bytes 196616 | tf_op jit(solution)/shard_map/ppermute | solution.py:320
  9.6 0.0 collective-permute-done.1.after_ref
  9.6 0.9 %collective-permute-done.before_ref = bf16[2,1,64,256]{3,2,1,0:T(8,128)(2,1)S(1)} collective-permute-done((bf16[2,1,64,256]{3,2,1,0:T(8,128)(2,1)S(1)}, bf16[2,1,64,256]{3,2,1,0:T(8,128)(2,1)S(1)}, u32[]{:S(2)}, u32[]{:S(2)}) %collective-permute-start) | collective-permute-done | bytes 65568 | tf_op jit(solution)/shard_map/ppermute | solution.py:320
  10.5 1.0 %pad_maximum_fusion.refs_1_.refs_5_.refs_9_ = bf16[1,10,64,256]{3,2,1,0:T(8,128)(2,1)S(1)} fusion(bf16[1,1,64,256]{3,2,1,0:T(8,128)(2,1)S(1)} %slice.27, bf16[1,8,64,256]{3,2,1,0:T(8,128)(2,1)} %param.11, bf16[1,1,64,256]{3,2,1,0:T(8,128)(2,1)S(1)} %slice.26), kind=kLoop, calls=%fused_computation | loop fusion | flops 327680 | bytes 655360 | tf_op jit(solution)/shard_map/concatenate | solution.py:322
  11.5 0.1 collective-permute-start.8
  11.6 2.0 %collective-permute-start.7 = (bf16[1,10,64,256]{3,2,1,0:T(8,128)(2,1)S(1)}, bf16[1,10,64,256]{3,2,1,0:T(8,128)(2,1)S(1)}, u32[]{:S(2)}, u32[]{:S(2)}) collective-permute-start(bf16[1,10,64,256]{3,2,1,0:T(8,128)(2,1)S(1)} %pad_maximum_fusion.refs_1_.refs_5_.refs_9_), channel_id=1, source_target_pairs={{0,16},{8,24},{16,0},{24,8},{1,17},{9,25},{17,1},{25,9},{2,18},{10... | collective-permute-start | bytes 983048 | tf_op jit(solution)/shard_map/ppermute | solution.py:326
  13.6 1.5 %collective-permute-start.6 = (bf16[1,10,64,256]{3,2,1,0:T(8,128)(2,1)S(1)}, bf16[1,10,64,256]{3,2,1,0:T(8,128)(2,1)S(1)}, u32[]{:S(2)}, u32[]{:S(2)}) collective-permute-start(bf16[1,10,64,256]{3,2,1,0:T(8,128)(2,1)S(1)} %pad_maximum_fusion.refs_1_.refs_5_.refs_9_), channel_id=1, source_target_pairs={{0,8},{8,0},{16,24},{24,16},{1,9},{9,1},{17,25},{25,17},{2,10},{10... | collective-permute-start | bytes 983048 | tf_op jit(solution)/shard_map/ppermute | solution.py:326
  15.7 0.0 copy-start
  15.7 0.9 %copy-done = bf16[8,64,256]{2,1,0:T(8,128)(2,1)S(1)} copy-done((bf16[8,64,256]{2,1,0:T(8,128)(2,1)S(1)}, bf16[8,64,256]{2,1,0:T(8,128)(2,1)}, u32[]{:S(2)}) %copy-start) | copy-done | bytes 262168
  16.7 0.0 copy-start.2
  16.7 1.8 %copy-done.2 = bf16[1,8,64,2816]{3,2,1,0:T(8,128)(2,1)S(1)} copy-done((bf16[1,8,64,2816]{3,2,1,0:T(8,128)(2,1)S(1)}, bf16[1,8,64,2816]{3,2,1,0:T(8,128)(2,1)}, u32[]{:S(2)}) %copy-start.2) | copy-done | bytes 2883608
  18.5 0.0 copy-start.3
  18.5 0.9 %copy-done.3 = bf16[44,4,44,4]{2,3,1,0:T(4,128)(2,1)S(1)} copy-done((bf16[44,4,44,4]{2,3,1,0:T(4,128)(2,1)S(1)}, bf16[44,4,44,4]{2,3,1,0:T(4,128)(2,1)}, u32[]{:S(2)}) %copy-start.3) | copy-done | bytes 61976
  19.4 13.2 %mix_shifted.1 = (bf16[8,2,256,1408]{3,2,1,0:T(8,128)(2,1)S(1)}, bf16[176,192]{1,0:T(8,128)(2,1)S(1)}) custom-call(bf16[8,64,2816]{2,1,0:T(8,128)(2,1)S(1)} %bitcast.6, bf16[8,64,256]{2,1,0:T(8,128)(2,1)S(1)} %copy-done, bf16[8,64,256]{2,1,0:T(8,128)(2,1)S(1)} %copy-done, bf16[8,64,256]{2,1,0:T(8,128)(2,1)S(1)} %copy-done, ...), custom_call_target="tpu_custom_call" | custom-call | flops 960000000 | bytes 1440000 | tf_op jit(solution)/shard_map/mix_shifted/pallas_call | solution.py:229
  32.6 0.0 collective-permute-done.3.refs_2_
  32.7 0.6 collective-permute-start.5
  33.3 0.0 collective-permute-done.2.refs_1_
  33.3 0.2 collective-permute-start.4
  33.5 0.0 collective-permute-done.8.refs_4_.refs_8_.refs_12_
  33.5 0.0 collective-permute-done.7.refs_3_.refs_7_.refs_11_
  33.5 1.4 %collective-permute-done.6.refs_2_.refs_6_.refs_10_ = bf16[1,10,64,256]{3,2,1,0:T(8,128)(2,1)S(1)} collective-permute-done((bf16[1,10,64,256]{3,2,1,0:T(8,128)(2,1)S(1)}, bf16[1,10,64,256]{3,2,1,0:T(8,128)(2,1)S(1)}, u32[]{:S(2)}, u32[]{:S(2)}) %collective-permute-start.6) | collective-permute-done | bytes 327712 | tf_op jit(solution)/shard_map/ppermute | solution.py:326
  34.9 0.0 copy-start.5
  34.9 1.1 %copy-done.5 = bf16[8,16,2816]{2,1,0:T(8,128)(2,1)S(1)} copy-done((bf16[8,16,2816]{2,1,0:T(8,128)(2,1)S(1)}, bf16[8,16,2816]{2,1,0:T(8,128)(2,1)}, u32[]{:S(2)}) %copy-start.5) | copy-done | bytes 720920
  36.0 0.0 copy-start.1
  36.0 11.2 %mix_direct.1.mixed_ref = bf16[8,2,256,1408]{3,2,1,0:T(8,128)(2,1)S(1)} custom-call(bf16[8,16,2816]{2,1,0:T(8,128)(2,1)S(1)} %copy-done.5, bf16[1,10,64,256]{3,2,1,0:T(8,128)(2,1)S(1)} %pad_maximum_fusion.refs_1_.refs_5_.refs_9_, bf16[1,10,64,256]{3,2,1,0:T(8,128)(2,1)S(1)} %collective-permute-done.6.refs_2_.refs_6_.refs_10_, ...), custom_call_target="tpu_custom_call" | custom-call | flops 9600000000 | bytes 14400000 | tf_op jit(solution)/shard_map/mix_direct/pallas_call | solution.py:255
  47.2 0.0 copy-start.4
  47.2 0.0 collective-permute-done.5.refs_4_
  47.2 0.0 collective-permute-done.4.refs_3_
  47.2 0.0 copy-done.1
  47.2 5.7 %close_direct.1 = (bf16[8,16,256]{2,1,0:T(8,128)(2,1)S(1)}, bf16[8,16,256]{2,1,0:T(8,128)(2,1)S(1)}, bf16[8,16,256]{2,1,0:T(8,128)(2,1)S(1)}, bf16[8,16,256]{2,1,0:T(8,128)(2,1)S(1)}) custom-call(bf16[8,2,256,1408]{3,2,1,0:T(8,128)(2,1)S(1)} %mix_direct.1.mixed_ref, bf16[8,16,2816]{2,1,0:T(8,128)(2,1)S(1)} %copy-done.1, ...), custom_call_target="tpu_custom_call" | custom-call | flops 2400000000 | bytes 14400000 | tf_op jit(solution)/shard_map/close_direct/pallas_call | solution.py:282
  53.0 1.5 %collective-permute-start.9 = (bf16[8,16,256]{2,1,0:T(8,128)(2,1)S(1)}, bf16[8,16,256]{2,1,0:T(8,128)(2,1)S(1)}, u32[]{:S(2)}, u32[]{:S(2)}) collective-permute-start(bf16[8,16,256]{2,1,0:T(8,128)(2,1)S(1)} %get-tuple-element.14), channel_id=1, source_target_pairs={{0,8},{8,0},{16,24},{24,16},{1,9},{9,1},{17,25},{25,17},{2,10},{10... | collective-permute-start | bytes 196616 | tf_op jit(solution)/shard_map/ppermute | solution.py:338
  54.5 0.5 collective-permute-start.10
  55.0 1.5 %collective-permute-start.11 = (bf16[8,16,256]{2,1,0:T(8,128)(2,1)S(1)}, bf16[8,16,256]{2,1,0:T(8,128)(2,1)S(1)}, u32[]{:S(2)}, u32[]{:S(2)}) collective-permute-start(bf16[8,16,256]{2,1,0:T(8,128)(2,1)S(1)} %get-tuple-element.16), channel_id=1, source_target_pairs={{0,24},{8,16},{16,8},{24,0},{1,25},{9,17},{17,9},{25,1},{2,26},{10... | collective-permute-start | bytes 196616 | tf_op jit(solution)/shard_map/ppermute | solution.py:338
  56.5 5.8 %close_shifted.1.shifted_ref = f32[8,64,256]{2,1,0:T(8,128)S(1)} custom-call(bf16[8,2,256,1408]{3,2,1,0:T(8,128)(2,1)S(1)} %get-tuple-element.11.mixed_ref, bf16[8,16,2816]{2,1,0:T(8,128)(2,1)S(1)} %copy-done.1, bf16[8,16,2816]{2,1,0:T(8,128)(2,1)S(1)} %collective-permute-done.2.refs_1_, bf16[8,16,2816]{2,1,0:T(8,128)(2,1)S(1)} %collective-permute-done.3.refs_2_, ...), custom_call_target="tpu_custom_call" | custom-call | flops 2400000000 | bytes 14400000 | tf_op jit(solution)/shard_map/close_shifted/pallas_call | solution.py:282
  62.3 0.0 collective-permute-done.9.refs_1_
  62.3 0.0 collective-permute-done.10.refs_2_
  62.3 0.0 collective-permute-done.11.refs_3_
  62.3 0.0 copy-done.4
  62.3 1.6 %combine.1 = bf16[1,2,8,64,256]{4,3,2,1,0:T(8,128)(2,1)} custom-call(s32[8]{0:T(128)S(1)} %copy-done.4, f32[1]{0:T(128)S(6)} %div.3.turn_ref, f32[8,64,256]{2,1,0:T(8,128)S(1)} %close_shifted.1.shifted_ref, bf16[8,16,256]{2,1,0:T(8,128)(2,1)S(1)} %get-tuple-element.13.refs_0_, bf16[8,16,256]{2,1,0:T(8,128)(2,1)S(1)} %collective-permute-done.9.refs_1_, ...), custom_call_target="tpu_custom_call" | custom-call | flops 800000 | bytes 1600000 | tf_op jit(solution)/shard_map/combine/pallas_call | solution.py:297
  (4 shorter events, 0.1 us)
Async XLA Ops:
  0.0 32.6 %collective-permute-start.3 = (bf16[8,16,2816]{2,1,0:T(8,128)(2,1)}, bf16[8,16,2816]{2,1,0:T(8,128)(2,1)S(1)}, u32[]{:S(2)}, u32[]{:S(2)}) collective-permute-start(bf16[8,16,2816]{2,1,0:T(8,128)(2,1)} %refs_0_.5), channel_id=1, source_target_pairs={{0,16},{8,24},{16,0},{24,8},{1,17},{9,25},{17,1},{25,9},{2,18},{10... | collective-permute-start | bytes 2162696 | tf_op jit(solution)/shard_map/ppermute | solution.py:325
  3.0 30.3 %collective-permute-start.2 = (bf16[8,16,2816]{2,1,0:T(8,128)(2,1)}, bf16[8,16,2816]{2,1,0:T(8,128)(2,1)S(1)}, u32[]{:S(2)}, u32[]{:S(2)}) collective-permute-start(bf16[8,16,2816]{2,1,0:T(8,128)(2,1)} %refs_0_.5), channel_id=1, source_target_pairs={{0,8},{8,0},{16,24},{24,16},{1,9},{9,1},{17,25},{25,17},{2,10},{10... | collective-permute-start | bytes 2162696 | tf_op jit(solution)/shard_map/ppermute | solution.py:325
  5.3 4.3 %collective-permute-start.1 = (bf16[2,1,64,256]{3,2,1,0:T(8,128)(2,1)S(1)}, bf16[2,1,64,256]{3,2,1,0:T(8,128)(2,1)S(1)}, u32[]{:S(2)}, u32[]{:S(2)}) collective-permute-start(bf16[2,1,64,256]{3,2,1,0:T(8,128)(2,1)S(1)} %get-tuple-element.17), channel_id=1, source_target_pairs={{1,0},{2,1},{3,2},{4,3},{5,4},{6,5},{7,6},{9,8},{10,9},{11,10},{12... | collective-permute-start | bytes 196616 | tf_op jit(solution)/shard_map/ppermute | solution.py:321
  6.6 3.9 %collective-permute-start = (bf16[2,1,64,256]{3,2,1,0:T(8,128)(2,1)S(1)}, bf16[2,1,64,256]{3,2,1,0:T(8,128)(2,1)S(1)}, u32[]{:S(2)}, u32[]{:S(2)}) collective-permute-start(bf16[2,1,64,256]{3,2,1,0:T(8,128)(2,1)S(1)} %get-tuple-element.18), channel_id=1, source_target_pairs={{0,1},{1,2},{2,3},{3,4},{4,5},{5,6},{6,7},{8,9},{9,10},{10,11},{11... | collective-permute-start | bytes 196616 | tf_op jit(solution)/shard_map/ppermute | solution.py:320
  11.5 22.0 %collective-permute-start.8 = (bf16[1,10,64,256]{3,2,1,0:T(8,128)(2,1)S(1)}, bf16[1,10,64,256]{3,2,1,0:T(8,128)(2,1)S(1)}, u32[]{:S(2)}, u32[]{:S(2)}) collective-permute-start(bf16[1,10,64,256]{3,2,1,0:T(8,128)(2,1)S(1)} %pad_maximum_fusion.refs_1_.refs_5_.refs_9_), channel_id=1, source_target_pairs={{0,24},{8,16},{16,8},{24,0},{1,25},{9,17},{17,9},{25,1},{2,26},{10... | collective-permute-start | bytes 983048 | tf_op jit(solution)/shard_map/ppermute | solution.py:326
  11.6 21.9 %collective-permute-start.7 = (bf16[1,10,64,256]{3,2,1,0:T(8,128)(2,1)S(1)}, bf16[1,10,64,256]{3,2,1,0:T(8,128)(2,1)S(1)}, u32[]{:S(2)}, u32[]{:S(2)}) collective-permute-start(bf16[1,10,64,256]{3,2,1,0:T(8,128)(2,1)S(1)} %pad_maximum_fusion.refs_1_.refs_5_.refs_9_), channel_id=1, source_target_pairs={{0,16},{8,24},{16,0},{24,8},{1,17},{9,25},{17,1},{25,9},{2,18},{10... | collective-permute-start | bytes 983048 | tf_op jit(solution)/shard_map/ppermute | solution.py:326
  13.6 21.3 %collective-permute-start.6 = (bf16[1,10,64,256]{3,2,1,0:T(8,128)(2,1)S(1)}, bf16[1,10,64,256]{3,2,1,0:T(8,128)(2,1)S(1)}, u32[]{:S(2)}, u32[]{:S(2)}) collective-permute-start(bf16[1,10,64,256]{3,2,1,0:T(8,128)(2,1)S(1)} %pad_maximum_fusion.refs_1_.refs_5_.refs_9_), channel_id=1, source_target_pairs={{0,8},{8,0},{16,24},{24,16},{1,9},{9,1},{17,25},{25,17},{2,10},{10... | collective-permute-start | bytes 983048 | tf_op jit(solution)/shard_map/ppermute | solution.py:326
  15.7 1.0 %copy-start = (bf16[8,64,256]{2,1,0:T(8,128)(2,1)S(1)}, bf16[8,64,256]{2,1,0:T(8,128)(2,1)}, u32[]{:S(2)}) copy-start(bf16[8,64,256]{2,1,0:T(8,128)(2,1)} %s2_ref.1) | copy-start | bytes 786436
  16.7 1.8 %copy-start.2 = (bf16[1,8,64,2816]{3,2,1,0:T(8,128)(2,1)S(1)}, bf16[1,8,64,2816]{3,2,1,0:T(8,128)(2,1)}, u32[]{:S(2)}) copy-start(bf16[1,8,64,2816]{3,2,1,0:T(8,128)(2,1)} %param.10) | copy-start | bytes 8650756
  18.5 0.9 %copy-start.3 = (bf16[44,4,44,4]{2,3,1,0:T(4,128)(2,1)S(1)}, bf16[44,4,44,4]{2,3,1,0:T(4,128)(2,1)}, u32[]{:S(2)}) copy-start(bf16[44,4,44,4]{2,3,1,0:T(4,128)(2,1)} %param.13) | copy-start | bytes 185860
  32.7 14.5 %collective-permute-start.5 = (bf16[4,16,2816]{2,1,0:T(8,128)(2,1)S(1)}, bf16[4,16,2816]{2,1,0:T(8,128)(2,1)S(1)}, u32[]{:S(2)}, u32[]{:S(2)}) collective-permute-start(bf16[4,16,2816]{2,1,0:T(8,128)(2,1)S(1)} %slice.25), channel_id=1, source_target_pairs={{0,8},{8,0},{16,24},{24,16},{1,9},{9,1},{17,25},{25,17},{2,10},{10... | collective-permute-start | bytes 1081352 | tf_op jit(solution)/shard_map/ppermute | solution.py:327
  33.3 13.9 %collective-permute-start.4 = (bf16[4,16,2816]{2,1,0:T(8,128)(2,1)S(1)}, bf16[4,16,2816]{2,1,0:T(8,128)(2,1)S(1)}, u32[]{:S(2)}, u32[]{:S(2)}) collective-permute-start(bf16[4,16,2816]{2,1,0:T(8,128)(2,1)S(1)} %slice.24), channel_id=1, source_target_pairs={{0,16},{8,24},{16,0},{24,8},{1,17},{9,25},{17,1},{25,9},{2,18},{10... | collective-permute-start | bytes 1081352 | tf_op jit(solution)/shard_map/ppermute | solution.py:327
  34.9 1.1 %copy-start.5 = (bf16[8,16,2816]{2,1,0:T(8,128)(2,1)S(1)}, bf16[8,16,2816]{2,1,0:T(8,128)(2,1)}, u32[]{:S(2)}) copy-start(bf16[8,16,2816]{2,1,0:T(8,128)(2,1)} %refs_0_.4) | copy-start | bytes 2162692
  36.0 11.2 %copy-start.1 = (bf16[8,16,2816]{2,1,0:T(8,128)(2,1)S(1)}, bf16[8,16,2816]{2,1,0:T(8,128)(2,1)}, u32[]{:S(2)}) copy-start(bf16[8,16,2816]{2,1,0:T(8,128)(2,1)} %refs_0_.5) | copy-start | bytes 2162692
  47.2 15.2 %copy-start.4 = (s32[8]{0:T(128)S(1)}, s32[8]{0:T(128)}, u32[]{:S(2)}) copy-start(s32[8]{0:T(128)} %dims_ref.1) | copy-start | bytes 100
  53.0 9.3 %collective-permute-start.9 = (bf16[8,16,256]{2,1,0:T(8,128)(2,1)S(1)}, bf16[8,16,256]{2,1,0:T(8,128)(2,1)S(1)}, u32[]{:S(2)}, u32[]{:S(2)}) collective-permute-start(bf16[8,16,256]{2,1,0:T(8,128)(2,1)S(1)} %get-tuple-element.14), channel_id=1, source_target_pairs={{0,8},{8,0},{16,24},{24,16},{1,9},{9,1},{17,25},{25,17},{2,10},{10... | collective-permute-start | bytes 196616 | tf_op jit(solution)/shard_map/ppermute | solution.py:338
  54.5 7.8 %collective-permute-start.10 = (bf16[8,16,256]{2,1,0:T(8,128)(2,1)S(1)}, bf16[8,16,256]{2,1,0:T(8,128)(2,1)S(1)}, u32[]{:S(2)}, u32[]{:S(2)}) collective-permute-start(bf16[8,16,256]{2,1,0:T(8,128)(2,1)S(1)} %get-tuple-element.15), channel_id=1, source_target_pairs={{0,16},{8,24},{16,0},{24,8},{1,17},{9,25},{17,1},{25,9},{2,18},{10... | collective-permute-start | bytes 196616 | tf_op jit(solution)/shard_map/ppermute | solution.py:338
  55.0 7.3 %collective-permute-start.11 = (bf16[8,16,256]{2,1,0:T(8,128)(2,1)S(1)}, bf16[8,16,256]{2,1,0:T(8,128)(2,1)S(1)}, u32[]{:S(2)}, u32[]{:S(2)}) collective-permute-start(bf16[8,16,256]{2,1,0:T(8,128)(2,1)S(1)} %get-tuple-element.16), channel_id=1, source_target_pairs={{0,24},{8,16},{16,8},{24,0},{1,25},{9,17},{17,9},{25,1},{2,26},{10... | collective-permute-start | bytes 196616 | tf_op jit(solution)/shard_map/ppermute | solution.py:338

commit v3 on v2

--- a/solution.py
+++ b/solution.py
@@ -10,6 +10,9 @@
 
 BF16, F32 = jnp.bfloat16, jnp.float32
 VMEM_LIMIT = 24 << 20
+UNROLL = 2
+CA = 256
+CB = 256
 
 
 def swap(x):
@@ -47,12 +50,12 @@
             for u in range(pairs // 2):
                 first = 4 * u + e
                 for t in range(2):
-                    x = o2[group][t, pl.ds(first, 16, stride=stride), :]
-                    y = o2[group][t, pl.ds(first + 2, 16, stride=stride), :]
+                    x = o2[group][t, pl.ds(first, 16, stride=stride), :].astype(BF16)
+                    y = o2[group][t, pl.ds(first + 2, 16, stride=stride), :].astype(BF16)
                     row = t * 128 + group * 16
                     cols = slice(u * 128, (u + 1) * 128)
-                    out_ref[0, e, row : row + 16, cols] = jnp.where(lane, x, swap(y)).astype(BF16)
-                    out_ref[0, e, row + 64 : row + 80, cols] = jnp.where(lane, swap(x), y).astype(BF16)
+                    out_ref[0, e, row : row + 16, cols] = jnp.where(lane, x, swap(y))
+                    out_ref[0, e, row + 64 : row + 80, cols] = jnp.where(lane, swap(x), y)
 
     for group in range(4):
         contract(group)
@@ -90,7 +93,6 @@
     @pl.when(pl.program_id(0) == 0)
     def _():
         g[...] = jnp.zeros_like(g)
-        bd[...] = jnp.zeros_like(bd)
         regroup_mpo(mpo_ref, mx_ref, pairs)
 
     spread(l_ref, g, 64, pairs)
@@ -102,7 +104,7 @@
         u, h = pr // 2, pr % 2
         for c in range(3):
             both = jnp.concatenate([e[c * 8 : c * 8 + 8], o[c * 8 : c * 8 + 8]], 0)
-            lq[c, u * 16 : (u + 1) * 16, h * 128 : (h + 1) * 128] = both.astype(BF16)
+            lq[c, (16 * h + u) * 16 : (16 * h + u + 1) * 16, :] = both.astype(BF16)
     for c, s_ref in enumerate((s0_ref, s1_ref, s2_ref)):
         for t in range(2):
             x = s_ref[0, :, t * 128 : (t + 1) * 128].astype(F32)
@@ -115,13 +117,15 @@
             for half, here, there in ((0, x, y), (1, y, x)):
                 first = jnp.where(lane, here, z).astype(BF16)
                 second = jnp.where(lane, z, there).astype(BF16)
-                for b in range(4):
-                    cols = slice((b // 2) * 128, (b // 2) * 128 + 128)
-                    bd[c * 4 + 2 * t + half, b * 64 : b * 64 + 64, cols] = first if b % 2 == 0 else second
+                bd[c * 4 + 2 * t + half, 0:64, :] = first
+                bd[c * 4 + 2 * t + half, 64:128, :] = second
     for c in range(3):
         for p in range(4):
-            y = jnp.dot(lq[c], bd[c * 4 + p], preferred_element_type=F32).astype(BF16)
-            temp[:, p * 48 + c * 16 : p * 48 + c * 16 + 16, :] = y.reshape(16, 16, 256)
+            for n in range(512 // CA):
+                y = jnp.dot(lq[c, n * CA : (n + 1) * CA, :], bd[c * 4 + p], preferred_element_type=F32).astype(BF16)
+                u, h = n * CA // 16 % 16, n * CA // 256
+                rows = slice(p * 48 + c * 16, p * 48 + c * 16 + 16)
+                temp[u : u + CA // 16, rows, h * 128 : (h + 1) * 128] = y.reshape(CA // 16, 16, 128)
     finish_mix(mx_ref, temp, o2, out_ref, pairs)
 
 
@@ -153,40 +157,51 @@
                     ex[(c * 4 + 2 * t + 1) * quads + mg, 0:64, cols] = jnp.where(lane, swap(x), y).astype(BF16)
         for p in range(4):
             for mg in range(quads):
-                y = jnp.dot(lq[c], ex[(c * 4 + p) * quads + mg], preferred_element_type=F32).astype(BF16)
-                temp[mg * rows : (mg + 1) * rows, p * 48 + c * 16 : p * 48 + c * 16 + 16, :] = y.reshape(rows, 16, 256)
+                size = min(CB, rows * 16)
+                for n in range(rows * 16 // size):
+                    some = lq[c, n * size : (n + 1) * size, :]
+                    y = jnp.dot(some, ex[(c * 4 + p) * quads + mg], preferred_element_type=F32).astype(BF16)
+                    u = mg * rows + n * size // 16
+                    temp[u : u + size // 16, p * 48 + c * 16 : p * 48 + c * 16 + 16, :] = y.reshape(size // 16, 16, 256)
     finish_mix(mx_ref, temp, o2, out_ref, pairs)
 
 
-def close_kernel(pairs, spans, direct, count, mixed_ref, *refs):
-    pieces, outs, (rs, res, fin) = refs[:count], refs[count:-3], refs[-3:]
+def close_kernel(pairs, spans, direct, count, unroll, mixed_ref, *refs):
+    pieces, outs = refs[:count], refs[count : -3 * unroll]
+    scratch = refs[-3 * unroll :]
     lane = low_half()
 
-    def sector(parts, s):
-        for n, k, base in parts:
-            size = pieces[n].shape[1]
-            start = 0 if k is None else (lax.axis_index("mom") ^ k) * size
-            for t in range(pairs):
-                at = pl.multiple_of(start + t * 64, size)
-                rs[pl.ds(at, size), :] = pieces[n][s - base, :, t * 128 : (t + 1) * 128]
-        even = jnp.dot(mixed_ref[s, 0], rs[...], preferred_element_type=F32)
-        odd = jnp.dot(mixed_ref[s, 1], rs[...], preferred_element_type=F32)
-        res[...] = even + swap(odd)
-        for t in range(2):
-            x = res[pl.ds(2 * t, 64, stride=4), :]
-            y = res[pl.ds(2 * t + 1, 64, stride=4), :]
-            z = jnp.where(lane, x, swap(y))
-            cols = slice(t * 128, (t + 1) * 128)
-            if direct:
-                for k, out_ref in enumerate(outs):
-                    out_ref[s, :, cols] = z[k * 16 : (k + 1) * 16].astype(BF16)
-            else:
-                for k in range(4):
-                    fin[t, pl.ds(k, 16, stride=4), :] = z[k * 16 : (k + 1) * 16]
-                outs[0][s, :, cols] = fin[t]
+    def sectors(parts, lo, step):
+        first = lo + step * unroll
+        for i in range(unroll):
+            for n, k, base in parts:
+                size = pieces[n].shape[1]
+                start = 0 if k is None else (lax.axis_index("mom") ^ k) * size
+                for t in range(pairs):
+                    at = pl.multiple_of(start + t * 64, size)
+                    scratch[3 * i][pl.ds(at, size), :] = pieces[n][first + i - base, :, t * 128 : (t + 1) * 128]
+        for i in range(unroll):
+            rs, res = scratch[3 * i : 3 * i + 2]
+            even = jnp.dot(mixed_ref[first + i, 0], rs[...], preferred_element_type=F32)
+            odd = jnp.dot(mixed_ref[first + i, 1], rs[...], preferred_element_type=F32)
+            res[...] = even + swap(odd)
+        for i in range(unroll):
+            res, fin = scratch[3 * i + 1 : 3 * i + 3]
+            for t in range(2):
+                x = res[pl.ds(2 * t, 64, stride=4), :]
+                y = res[pl.ds(2 * t + 1, 64, stride=4), :]
+                z = jnp.where(lane, x, swap(y))
+                cols = slice(t * 128, (t + 1) * 128)
+                if direct:
+                    for k, out_ref in enumerate(outs):
+                        out_ref[first + i, :, cols] = z[k * 16 : (k + 1) * 16].astype(BF16)
+                else:
+                    for k in range(4):
+                        fin[t, pl.ds(k, 16, stride=4), :] = z[k * 16 : (k + 1) * 16]
+                    outs[0][first + i, :, cols] = fin[t]
 
     for lo, hi, parts in spans:
-        pl.loop(lo, hi)(functools.partial(sector, parts))
+        pl.loop(0, (hi - lo) // unroll)(functools.partial(sectors, parts, lo))
 
 
 def combine_kernel(dims_ref, turn_ref, shifted_ref, *refs):
@@ -238,7 +253,7 @@
             jax.ShapeDtypeStruct((sectors, 2, 256, lanes // 2), BF16),
             jax.ShapeDtypeStruct((wide, 48 * phys), BF16),
         ],
-        scratch_shapes=[pltpu.VMEM((64 * 24, 128), F32), pltpu.VMEM((3, 256, 256), BF16), pltpu.VMEM((12, 256, 256), BF16)]
+        scratch_shapes=[pltpu.VMEM((64 * 24, 128), F32), pltpu.VMEM((3, 512, 128), BF16), pltpu.VMEM((12, 128, 128), BF16)]
         + mix_scratch(wide, pairs),
         compiler_params=params(),
         cost_estimate=cost(sectors * 0.12e9, sectors * 0.18e6),
@@ -278,13 +293,14 @@
         parts = [(n, k, base) for n, (p, k, base) in enumerate(pieces) if base <= lo and hi <= base + p.shape[0]]
         spans.append((lo, hi, parts))
     rows, kind, count = (16, BF16, 4) if direct else (64, F32, 1)
+    unroll = UNROLL if all((hi - lo) % UNROLL == 0 for lo, hi, _ in spans) else 1
     vmem = pl.BlockSpec(memory_space=pltpu.VMEM)
     return pl.pallas_call(
-        functools.partial(close_kernel, lanes // 128, spans, direct, len(pieces)),
+        functools.partial(close_kernel, lanes // 128, spans, direct, len(pieces), unroll),
         in_specs=[vmem] * (1 + len(pieces)),
         out_specs=[vmem] * count,
         out_shape=[jax.ShapeDtypeStruct((sectors, rows, 256), kind)] * count,
-        scratch_shapes=[pltpu.VMEM((lanes // 2, 128), BF16), pltpu.VMEM((256, 128), F32), pltpu.VMEM((2, 64, 128), F32)],
+        scratch_shapes=[pltpu.VMEM((lanes // 2, 128), BF16), pltpu.VMEM((256, 128), F32), pltpu.VMEM((2, 64, 128), F32)] * unroll,
         compiler_params=params(),
         cost_estimate=cost(sectors * 0.3e9, sectors * 1.8e6),
         name="close_direct" if direct else "close_shifted",

time: 64.3 us -> 61.8 us (0.961)
  Pallas kernels: 37.5 us -> 34 us
  waiting for transfers between devices: 2.28 us -> 3.21 us
    pallas_call x2, Pallas kernels: 11.5 us -> 9.25 us  [close(): pl.pallas_call(functools.partial(close_kernel, lanes // 128, spans, direc...]
    ppermute x3, waiting for transfers between devices: 1.4 us -> 2.33 us  [shards(): sources = [own] + [hop[k](own) for k in (1, 2, 3)]]
    pallas_call x1, Pallas kernels: 13.2 us -> 12.3 us  [mix_shifted(): pl.pallas_call(functools.partial(shifted_kernel, pairs), grid=(sectors,),...]
  transfers between devices with their start and end apart: 12 -> 12, of which waited for: 2 -> 3; matrix products, arithmetic and copies ran while one was open for 3% -> 3% of each run, Pallas kernels for 47% -> 45%
where the time goes in v3:
time: 61.8 us; the launch traced here: 61.4 us
  Pallas kernels  34 us (55%)
  starting transfers between devices  16.8 us (27%)
  local copies, waits for them, and re-layouts  4.86 us (8%)
  waiting for transfers between devices  3.21 us (5%)
  other arithmetic  1.81 us (3%)
  between operations  0.82 us (1%)
    pallas_call x1, Pallas kernels, mix_shifted(): pl.pallas_call(functools.partial(shifted_kernel, pairs), grid=(sectors,),...  12.3 us
    pallas_call x1, Pallas kernels, mix_direct(): pl.pallas_call(functools.partial(direct_kernel, pairs, rows, len(sources)...  10.9 us
    pallas_call x2, Pallas kernels, close(): pl.pallas_call(functools.partial(close_kernel, lanes // 128, spans, direc...  9.25 us
    unnamed x12, local copies, waits for them, and re-layouts  4.8 us
    ppermute x2, starting transfers between devices, shards(): right1, right2 = (hop[1](right_env), hop[2](right_env))  4.46 us
    ppermute x3, starting transfers between devices, shards(): parts = [parts[0]] + [hop[k](parts[k]) for k in (1, 2, 3)]  3.65 us
    ppermute x3, starting transfers between devices, shards(): sources = [own] + [hop[k](own) for k in (1, 2, 3)]  3.55 us
    ppermute x1, starting transfers between devices, shards(): before = lax.ppermute(stacked[:, sectors - 1:], 'sec', up)  3.03 us
  transfers between devices with their start and end apart: 12, of which 3 were waited for; matrix products, arithmetic and copies ran while one was open for 3% of the time, Pallas kernels for 45%

profile of v3, /device:TPU:0, one launch (start us, length us, event | category | flops | bytes accessed | tf_op | source)
XLA Modules:
  0.0 61.4 jit_solution(9216449821754066395)
XLA Ops:
  0.0 3.0 %collective-permute-start.3 = (bf16[8,16,2816]{2,1,0:T(8,128)(2,1)}, bf16[8,16,2816]{2,1,0:T(8,128)(2,1)S(1)}, u32[]{:S(2)}, u32[]{:S(2)}) collective-permute-start(bf16[8,16,2816]{2,1,0:T(8,128)(2,1)} %refs_0_.5), channel_id=1, source_target_pairs={{0,16},{8,24},{16,0},{24,8},{1,17},{9,25},{17,1},{25,9},{2,18},{10... | collective-permute-start | bytes 2162696 | tf_op jit(solution)/shard_map/ppermute | solution.py:341
  3.0 1.5 %collective-permute-start.2 = (bf16[8,16,2816]{2,1,0:T(8,128)(2,1)}, bf16[8,16,2816]{2,1,0:T(8,128)(2,1)S(1)}, u32[]{:S(2)}, u32[]{:S(2)}) collective-permute-start(bf16[8,16,2816]{2,1,0:T(8,128)(2,1)} %refs_0_.5), channel_id=1, source_target_pairs={{0,8},{8,0},{16,24},{24,16},{1,9},{9,1},{17,25},{25,17},{2,10},{10... | collective-permute-start | bytes 2162696 | tf_op jit(solution)/shard_map/ppermute | solution.py:341
  4.5 0.8 %pad_maximum_fusion.1 = (bf16[2,1,64,256]{3,2,1,0:T(8,128)(2,1)S(1)}, bf16[2,1,64,256]{3,2,1,0:T(8,128)(2,1)S(1)}) fusion(bf16[1,8,64,256]{3,2,1,0:T(8,128)(2,1)} %bitcast.5, bf16[1,8,64,256]{3,2,1,0:T(8,128)(2,1)} %param.11), kind=kLoop, calls=%fused_computation.1 | loop fusion | flops 65536 | bytes 655360 | tf_op jit(solution)/shard_map/stack | solution.py:335
  5.3 1.3 %collective-permute-start.1 = (bf16[2,1,64,256]{3,2,1,0:T(8,128)(2,1)S(1)}, bf16[2,1,64,256]{3,2,1,0:T(8,128)(2,1)S(1)}, u32[]{:S(2)}, u32[]{:S(2)}) collective-permute-start(bf16[2,1,64,256]{3,2,1,0:T(8,128)(2,1)S(1)} %get-tuple-element.17), channel_id=1, source_target_pairs={{1,0},{2,1},{3,2},{4,3},{5,4},{6,5},{7,6},{9,8},{10,9},{11,10},{12... | collective-permute-start | bytes 196616 | tf_op jit(solution)/shard_map/ppermute | solution.py:337
  6.6 3.0 %collective-permute-start = (bf16[2,1,64,256]{3,2,1,0:T(8,128)(2,1)S(1)}, bf16[2,1,64,256]{3,2,1,0:T(8,128)(2,1)S(1)}, u32[]{:S(2)}, u32[]{:S(2)}) collective-permute-start(bf16[2,1,64,256]{3,2,1,0:T(8,128)(2,1)S(1)} %get-tuple-element.18), channel_id=1, source_target_pairs={{0,1},{1,2},{2,3},{3,4},{4,5},{5,6},{6,7},{8,9},{9,10},{10,11},{11... | collective-permute-start | bytes 196616 | tf_op jit(solution)/shard_map/ppermute | solution.py:336
  9.6 0.0 collective-permute-done.1.after_ref
  9.6 0.9 %collective-permute-done.before_ref = bf16[2,1,64,256]{3,2,1,0:T(8,128)(2,1)S(1)} collective-permute-done((bf16[2,1,64,256]{3,2,1,0:T(8,128)(2,1)S(1)}, bf16[2,1,64,256]{3,2,1,0:T(8,128)(2,1)S(1)}, u32[]{:S(2)}, u32[]{:S(2)}) %collective-permute-start) | collective-permute-done | bytes 65568 | tf_op jit(solution)/shard_map/ppermute | solution.py:336
  10.5 1.0 %pad_maximum_fusion.refs_1_.refs_5_.refs_9_ = bf16[1,10,64,256]{3,2,1,0:T(8,128)(2,1)S(1)} fusion(bf16[1,1,64,256]{3,2,1,0:T(8,128)(2,1)S(1)} %slice.27, bf16[1,8,64,256]{3,2,1,0:T(8,128)(2,1)} %param.11, bf16[1,1,64,256]{3,2,1,0:T(8,128)(2,1)S(1)} %slice.26), kind=kLoop, calls=%fused_computation | loop fusion | flops 327680 | bytes 655360 | tf_op jit(solution)/shard_map/concatenate | solution.py:338
  11.5 0.1 collective-permute-start.8
  11.6 2.0 %collective-permute-start.7 = (bf16[1,10,64,256]{3,2,1,0:T(8,128)(2,1)S(1)}, bf16[1,10,64,256]{3,2,1,0:T(8,128)(2,1)S(1)}, u32[]{:S(2)}, u32[]{:S(2)}) collective-permute-start(bf16[1,10,64,256]{3,2,1,0:T(8,128)(2,1)S(1)} %pad_maximum_fusion.refs_1_.refs_5_.refs_9_), channel_id=1, source_target_pairs={{0,16},{8,24},{16,0},{24,8},{1,17},{9,25},{17,1},{25,9},{2,18},{10... | collective-permute-start | bytes 983048 | tf_op jit(solution)/shard_map/ppermute | solution.py:342
  13.6 1.5 %collective-permute-start.6 = (bf16[1,10,64,256]{3,2,1,0:T(8,128)(2,1)S(1)}, bf16[1,10,64,256]{3,2,1,0:T(8,128)(2,1)S(1)}, u32[]{:S(2)}, u32[]{:S(2)}) collective-permute-start(bf16[1,10,64,256]{3,2,1,0:T(8,128)(2,1)S(1)} %pad_maximum_fusion.refs_1_.refs_5_.refs_9_), channel_id=1, source_target_pairs={{0,8},{8,0},{16,24},{24,16},{1,9},{9,1},{17,25},{25,17},{2,10},{10... | collective-permute-start | bytes 983048 | tf_op jit(solution)/shard_map/ppermute | solution.py:342
  15.7 0.0 copy-start
  15.7 0.9 %copy-done = bf16[8,64,256]{2,1,0:T(8,128)(2,1)S(1)} copy-done((bf16[8,64,256]{2,1,0:T(8,128)(2,1)S(1)}, bf16[8,64,256]{2,1,0:T(8,128)(2,1)}, u32[]{:S(2)}) %copy-start) | copy-done | bytes 262168
  16.7 0.0 copy-start.2
  16.7 1.8 %copy-done.2 = bf16[1,8,64,2816]{3,2,1,0:T(8,128)(2,1)S(1)} copy-done((bf16[1,8,64,2816]{3,2,1,0:T(8,128)(2,1)S(1)}, bf16[1,8,64,2816]{3,2,1,0:T(8,128)(2,1)}, u32[]{:S(2)}) %copy-start.2) | copy-done | bytes 2883608
  18.5 0.0 copy-start.3
  18.5 0.9 %copy-done.3 = bf16[44,4,44,4]{2,3,1,0:T(4,128)(2,1)S(1)} copy-done((bf16[44,4,44,4]{2,3,1,0:T(4,128)(2,1)S(1)}, bf16[44,4,44,4]{2,3,1,0:T(4,128)(2,1)}, u32[]{:S(2)}) %copy-start.3) | copy-done | bytes 61976
  19.4 12.3 %mix_shifted.1 = (bf16[8,2,256,1408]{3,2,1,0:T(8,128)(2,1)S(1)}, bf16[176,192]{1,0:T(8,128)(2,1)S(1)}) custom-call(bf16[8,64,2816]{2,1,0:T(8,128)(2,1)S(1)} %bitcast.6, bf16[8,64,256]{2,1,0:T(8,128)(2,1)S(1)} %copy-done, bf16[8,64,256]{2,1,0:T(8,128)(2,1)S(1)} %copy-done, bf16[8,64,256]{2,1,0:T(8,128)(2,1)S(1)} %copy-done, ...), custom_call_target="tpu_custom_call" | custom-call | flops 960000000 | bytes 1440000 | tf_op jit(solution)/shard_map/mix_shifted/pallas_call | solution.py:244
  31.7 0.0 collective-permute-done.3.refs_2_
  31.7 0.6 collective-permute-start.5
  32.3 0.0 collective-permute-done.2.refs_1_
  32.4 0.2 collective-permute-start.4
  32.5 0.0 collective-permute-done.8.refs_4_.refs_8_.refs_12_
  32.5 0.8 %collective-permute-done.7.refs_3_.refs_7_.refs_11_ = bf16[1,10,64,256]{3,2,1,0:T(8,128)(2,1)S(1)} collective-permute-done((bf16[1,10,64,256]{3,2,1,0:T(8,128)(2,1)S(1)}, bf16[1,10,64,256]{3,2,1,0:T(8,128)(2,1)S(1)}, u32[]{:S(2)}, u32[]{:S(2)}) %collective-permute-start.7) | collective-permute-done | bytes 327712 | tf_op jit(solution)/shard_map/ppermute | solution.py:342
  33.4 1.5 %collective-permute-done.6.refs_2_.refs_6_.refs_10_ = bf16[1,10,64,256]{3,2,1,0:T(8,128)(2,1)S(1)} collective-permute-done((bf16[1,10,64,256]{3,2,1,0:T(8,128)(2,1)S(1)}, bf16[1,10,64,256]{3,2,1,0:T(8,128)(2,1)S(1)}, u32[]{:S(2)}, u32[]{:S(2)}) %collective-permute-start.6) | collective-permute-done | bytes 327712 | tf_op jit(solution)/shard_map/ppermute | solution.py:342
  34.9 0.0 copy-start.5
  34.9 1.1 %copy-done.5 = bf16[8,16,2816]{2,1,0:T(8,128)(2,1)S(1)} copy-done((bf16[8,16,2816]{2,1,0:T(8,128)(2,1)S(1)}, bf16[8,16,2816]{2,1,0:T(8,128)(2,1)}, u32[]{:S(2)}) %copy-start.5) | copy-done | bytes 720920
  36.0 0.0 copy-start.1
  36.0 10.9 %mix_direct.1.mixed_ref = bf16[8,2,256,1408]{3,2,1,0:T(8,128)(2,1)S(1)} custom-call(bf16[8,16,2816]{2,1,0:T(8,128)(2,1)S(1)} %copy-done.5, bf16[1,10,64,256]{3,2,1,0:T(8,128)(2,1)S(1)} %pad_maximum_fusion.refs_1_.refs_5_.refs_9_, bf16[1,10,64,256]{3,2,1,0:T(8,128)(2,1)S(1)} %collective-permute-done.6.refs_2_.refs_6_.refs_10_, ...), custom_call_target="tpu_custom_call" | custom-call | flops 9600000000 | bytes 14400000 | tf_op jit(solution)/shard_map/mix_direct/pallas_call | solution.py:270
  46.9 0.0 copy-start.4
  46.9 0.0 collective-permute-done.5.refs_4_
  46.9 0.0 collective-permute-done.4.refs_3_
  46.9 0.0 copy-done.1
  46.9 4.6 %close_direct.1 = (bf16[8,16,256]{2,1,0:T(8,128)(2,1)S(1)}, bf16[8,16,256]{2,1,0:T(8,128)(2,1)S(1)}, bf16[8,16,256]{2,1,0:T(8,128)(2,1)S(1)}, bf16[8,16,256]{2,1,0:T(8,128)(2,1)S(1)}) custom-call(bf16[8,2,256,1408]{3,2,1,0:T(8,128)(2,1)S(1)} %mix_direct.1.mixed_ref, bf16[8,16,2816]{2,1,0:T(8,128)(2,1)S(1)} %copy-done.1, ...), custom_call_target="tpu_custom_call" | custom-call | flops 2400000000 | bytes 14400000 | tf_op jit(solution)/shard_map/close_direct/pallas_call | solution.py:298
  51.5 2.1 %collective-permute-start.9 = (bf16[8,16,256]{2,1,0:T(8,128)(2,1)S(1)}, bf16[8,16,256]{2,1,0:T(8,128)(2,1)S(1)}, u32[]{:S(2)}, u32[]{:S(2)}) collective-permute-start(bf16[8,16,256]{2,1,0:T(8,128)(2,1)S(1)} %get-tuple-element.14), channel_id=1, source_target_pairs={{0,8},{8,0},{16,24},{24,16},{1,9},{9,1},{17,25},{25,17},{2,10},{10... | collective-permute-start | bytes 196616 | tf_op jit(solution)/shard_map/ppermute | solution.py:354
  53.6 0.5 collective-permute-start.10
  54.2 1.0 %collective-permute-start.11 = (bf16[8,16,256]{2,1,0:T(8,128)(2,1)S(1)}, bf16[8,16,256]{2,1,0:T(8,128)(2,1)S(1)}, u32[]{:S(2)}, u32[]{:S(2)}) collective-permute-start(bf16[8,16,256]{2,1,0:T(8,128)(2,1)S(1)} %get-tuple-element.16), channel_id=1, source_target_pairs={{0,24},{8,16},{16,8},{24,0},{1,25},{9,17},{17,9},{25,1},{2,26},{10... | collective-permute-start | bytes 196616 | tf_op jit(solution)/shard_map/ppermute | solution.py:354
  55.2 4.7 %close_shifted.1.shifted_ref = f32[8,64,256]{2,1,0:T(8,128)S(1)} custom-call(bf16[8,2,256,1408]{3,2,1,0:T(8,128)(2,1)S(1)} %get-tuple-element.11.mixed_ref, bf16[8,16,2816]{2,1,0:T(8,128)(2,1)S(1)} %copy-done.1, bf16[8,16,2816]{2,1,0:T(8,128)(2,1)S(1)} %collective-permute-done.2.refs_1_, bf16[8,16,2816]{2,1,0:T(8,128)(2,1)S(1)} %collective-permute-done.3.refs_2_, ...), custom_call_target="tpu_custom_call" | custom-call | flops 2400000000 | bytes 14400000 | tf_op jit(solution)/shard_map/close_shifted/pallas_call | solution.py:298
  59.8 0.0 collective-permute-done.9.refs_1_
  59.8 0.0 collective-permute-done.10.refs_2_
  59.9 0.0 collective-permute-done.11.refs_3_
  59.9 0.0 copy-done.4
  59.9 1.6 %combine.1 = bf16[1,2,8,64,256]{4,3,2,1,0:T(8,128)(2,1)} custom-call(s32[8]{0:T(128)S(1)} %copy-done.4, f32[1]{0:T(128)S(6)} %div.3.turn_ref, f32[8,64,256]{2,1,0:T(8,128)S(1)} %close_shifted.1.shifted_ref, bf16[8,16,256]{2,1,0:T(8,128)(2,1)S(1)} %get-tuple-element.13.refs_0_, bf16[8,16,256]{2,1,0:T(8,128)(2,1)S(1)} %collective-permute-done.9.refs_1_, ...), custom_call_target="tpu_custom_call" | custom-call | flops 800000 | bytes 1600000 | tf_op jit(solution)/shard_map/combine/pallas_call | solution.py:313
  (4 shorter events, 0.1 us)
Async XLA Ops:
  0.0 31.7 %collective-permute-start.3 = (bf16[8,16,2816]{2,1,0:T(8,128)(2,1)}, bf16[8,16,2816]{2,1,0:T(8,128)(2,1)S(1)}, u32[]{:S(2)}, u32[]{:S(2)}) collective-permute-start(bf16[8,16,2816]{2,1,0:T(8,128)(2,1)} %refs_0_.5), channel_id=1, source_target_pairs={{0,16},{8,24},{16,0},{24,8},{1,17},{9,25},{17,1},{25,9},{2,18},{10... | collective-permute-start | bytes 2162696 | tf_op jit(solution)/shard_map/ppermute | solution.py:341
  3.0 29.4 %collective-permute-start.2 = (bf16[8,16,2816]{2,1,0:T(8,128)(2,1)}, bf16[8,16,2816]{2,1,0:T(8,128)(2,1)S(1)}, u32[]{:S(2)}, u32[]{:S(2)}) collective-permute-start(bf16[8,16,2816]{2,1,0:T(8,128)(2,1)} %refs_0_.5), channel_id=1, source_target_pairs={{0,8},{8,0},{16,24},{24,16},{1,9},{9,1},{17,25},{25,17},{2,10},{10... | collective-permute-start | bytes 2162696 | tf_op jit(solution)/shard_map/ppermute | solution.py:341
  5.3 4.3 %collective-permute-start.1 = (bf16[2,1,64,256]{3,2,1,0:T(8,128)(2,1)S(1)}, bf16[2,1,64,256]{3,2,1,0:T(8,128)(2,1)S(1)}, u32[]{:S(2)}, u32[]{:S(2)}) collective-permute-start(bf16[2,1,64,256]{3,2,1,0:T(8,128)(2,1)S(1)} %get-tuple-element.17), channel_id=1, source_target_pairs={{1,0},{2,1},{3,2},{4,3},{5,4},{6,5},{7,6},{9,8},{10,9},{11,10},{12... | collective-permute-start | bytes 196616 | tf_op jit(solution)/shard_map/ppermute | solution.py:337
  6.6 3.9 %collective-permute-start = (bf16[2,1,64,256]{3,2,1,0:T(8,128)(2,1)S(1)}, bf16[2,1,64,256]{3,2,1,0:T(8,128)(2,1)S(1)}, u32[]{:S(2)}, u32[]{:S(2)}) collective-permute-start(bf16[2,1,64,256]{3,2,1,0:T(8,128)(2,1)S(1)} %get-tuple-element.18), channel_id=1, source_target_pairs={{0,1},{1,2},{2,3},{3,4},{4,5},{5,6},{6,7},{8,9},{9,10},{10,11},{11... | collective-permute-start | bytes 196616 | tf_op jit(solution)/shard_map/ppermute | solution.py:336
  11.5 21.0 %collective-permute-start.8 = (bf16[1,10,64,256]{3,2,1,0:T(8,128)(2,1)S(1)}, bf16[1,10,64,256]{3,2,1,0:T(8,128)(2,1)S(1)}, u32[]{:S(2)}, u32[]{:S(2)}) collective-permute-start(bf16[1,10,64,256]{3,2,1,0:T(8,128)(2,1)S(1)} %pad_maximum_fusion.refs_1_.refs_5_.refs_9_), channel_id=1, source_target_pairs={{0,24},{8,16},{16,8},{24,0},{1,25},{9,17},{17,9},{25,1},{2,26},{10... | collective-permute-start | bytes 983048 | tf_op jit(solution)/shard_map/ppermute | solution.py:342
  11.6 21.8 %collective-permute-start.7 = (bf16[1,10,64,256]{3,2,1,0:T(8,128)(2,1)S(1)}, bf16[1,10,64,256]{3,2,1,0:T(8,128)(2,1)S(1)}, u32[]{:S(2)}, u32[]{:S(2)}) collective-permute-start(bf16[1,10,64,256]{3,2,1,0:T(8,128)(2,1)S(1)} %pad_maximum_fusion.refs_1_.refs_5_.refs_9_), channel_id=1, source_target_pairs={{0,16},{8,24},{16,0},{24,8},{1,17},{9,25},{17,1},{25,9},{2,18},{10... | collective-permute-start | bytes 983048 | tf_op jit(solution)/shard_map/ppermute | solution.py:342
  13.6 21.3 %collective-permute-start.6 = (bf16[1,10,64,256]{3,2,1,0:T(8,128)(2,1)S(1)}, bf16[1,10,64,256]{3,2,1,0:T(8,128)(2,1)S(1)}, u32[]{:S(2)}, u32[]{:S(2)}) collective-permute-start(bf16[1,10,64,256]{3,2,1,0:T(8,128)(2,1)S(1)} %pad_maximum_fusion.refs_1_.refs_5_.refs_9_), channel_id=1, source_target_pairs={{0,8},{8,0},{16,24},{24,16},{1,9},{9,1},{17,25},{25,17},{2,10},{10... | collective-permute-start | bytes 983048 | tf_op jit(solution)/shard_map/ppermute | solution.py:342
  15.7 1.0 %copy-start = (bf16[8,64,256]{2,1,0:T(8,128)(2,1)S(1)}, bf16[8,64,256]{2,1,0:T(8,128)(2,1)}, u32[]{:S(2)}) copy-start(bf16[8,64,256]{2,1,0:T(8,128)(2,1)} %s2_ref.1) | copy-start | bytes 786436
  16.7 1.8 %copy-start.2 = (bf16[1,8,64,2816]{3,2,1,0:T(8,128)(2,1)S(1)}, bf16[1,8,64,2816]{3,2,1,0:T(8,128)(2,1)}, u32[]{:S(2)}) copy-start(bf16[1,8,64,2816]{3,2,1,0:T(8,128)(2,1)} %param.10) | copy-start | bytes 8650756
  18.5 0.9 %copy-start.3 = (bf16[44,4,44,4]{2,3,1,0:T(4,128)(2,1)S(1)}, bf16[44,4,44,4]{2,3,1,0:T(4,128)(2,1)}, u32[]{:S(2)}) copy-start(bf16[44,4,44,4]{2,3,1,0:T(4,128)(2,1)} %param.13) | copy-start | bytes 185860
  31.7 15.2 %collective-permute-start.5 = (bf16[4,16,2816]{2,1,0:T(8,128)(2,1)S(1)}, bf16[4,16,2816]{2,1,0:T(8,128)(2,1)S(1)}, u32[]{:S(2)}, u32[]{:S(2)}) collective-permute-start(bf16[4,16,2816]{2,1,0:T(8,128)(2,1)S(1)} %slice.25), channel_id=1, source_target_pairs={{0,8},{8,0},{16,24},{24,16},{1,9},{9,1},{17,25},{25,17},{2,10},{10... | collective-permute-start | bytes 1081352 | tf_op jit(solution)/shard_map/ppermute | solution.py:343
  32.4 14.5 %collective-permute-start.4 = (bf16[4,16,2816]{2,1,0:T(8,128)(2,1)S(1)}, bf16[4,16,2816]{2,1,0:T(8,128)(2,1)S(1)}, u32[]{:S(2)}, u32[]{:S(2)}) collective-permute-start(bf16[4,16,2816]{2,1,0:T(8,128)(2,1)S(1)} %slice.24), channel_id=1, source_target_pairs={{0,16},{8,24},{16,0},{24,8},{1,17},{9,25},{17,1},{25,9},{2,18},{10... | collective-permute-start | bytes 1081352 | tf_op jit(solution)/shard_map/ppermute | solution.py:343
  34.9 1.1 %copy-start.5 = (bf16[8,16,2816]{2,1,0:T(8,128)(2,1)S(1)}, bf16[8,16,2816]{2,1,0:T(8,128)(2,1)}, u32[]{:S(2)}) copy-start(bf16[8,16,2816]{2,1,0:T(8,128)(2,1)} %refs_0_.4) | copy-start | bytes 2162692
  36.0 10.9 %copy-start.1 = (bf16[8,16,2816]{2,1,0:T(8,128)(2,1)S(1)}, bf16[8,16,2816]{2,1,0:T(8,128)(2,1)}, u32[]{:S(2)}) copy-start(bf16[8,16,2816]{2,1,0:T(8,128)(2,1)} %refs_0_.5) | copy-start | bytes 2162692
  46.9 13.0 %copy-start.4 = (s32[8]{0:T(128)S(1)}, s32[8]{0:T(128)}, u32[]{:S(2)}) copy-start(s32[8]{0:T(128)} %dims_ref.1) | copy-start | bytes 100
  51.5 8.3 %collective-permute-start.9 = (bf16[8,16,256]{2,1,0:T(8,128)(2,1)S(1)}, bf16[8,16,256]{2,1,0:T(8,128)(2,1)S(1)}, u32[]{:S(2)}, u32[]{:S(2)}) collective-permute-start(bf16[8,16,256]{2,1,0:T(8,128)(2,1)S(1)} %get-tuple-element.14), channel_id=1, source_target_pairs={{0,8},{8,0},{16,24},{24,16},{1,9},{9,1},{17,25},{25,17},{2,10},{10... | collective-permute-start | bytes 196616 | tf_op jit(solution)/shard_map/ppermute | solution.py:354
  53.6 6.2 %collective-permute-start.10 = (bf16[8,16,256]{2,1,0:T(8,128)(2,1)S(1)}, bf16[8,16,256]{2,1,0:T(8,128)(2,1)S(1)}, u32[]{:S(2)}, u32[]{:S(2)}) collective-permute-start(bf16[8,16,256]{2,1,0:T(8,128)(2,1)S(1)} %get-tuple-element.15), channel_id=1, source_target_pairs={{0,16},{8,24},{16,0},{24,8},{1,17},{9,25},{17,1},{25,9},{2,18},{10... | collective-permute-start | bytes 196616 | tf_op jit(solution)/shard_map/ppermute | solution.py:354
  54.2 5.7 %collective-permute-start.11 = (bf16[8,16,256]{2,1,0:T(8,128)(2,1)S(1)}, bf16[8,16,256]{2,1,0:T(8,128)(2,1)S(1)}, u32[]{:S(2)}, u32[]{:S(2)}) collective-permute-start(bf16[8,16,256]{2,1,0:T(8,128)(2,1)S(1)} %get-tuple-element.16), channel_id=1, source_target_pairs={{0,24},{8,16},{16,8},{24,0},{1,25},{9,17},{17,9},{25,1},{2,26},{10... | collective-permute-start | bytes 196616 | tf_op jit(solution)/shard_map/ppermute | solution.py:354

commit v4 on v3

--- a/solution.py
+++ b/solution.py
@@ -10,7 +10,7 @@
 
 BF16, F32 = jnp.bfloat16, jnp.float32
 VMEM_LIMIT = 24 << 20
-UNROLL = 2
+UNROLL = 4
 CA = 256
 CB = 256
 
@@ -166,20 +166,30 @@
     finish_mix(mx_ref, temp, o2, out_ref, pairs)
 
 
-def close_kernel(pairs, spans, direct, count, unroll, mixed_ref, *refs):
+def close_kernel(pairs, layout, direct, unroll, mixed_ref, *refs):
+    count = len(layout)
     pieces, outs = refs[:count], refs[count : -3 * unroll]
     scratch = refs[-3 * unroll :]
     lane = low_half()
-
-    def sectors(parts, lo, step):
-        first = lo + step * unroll
-        for i in range(unroll):
-            for n, k, base in parts:
-                size = pieces[n].shape[1]
-                start = 0 if k is None else (lax.axis_index("mom") ^ k) * size
-                for t in range(pairs):
-                    at = pl.multiple_of(start + t * 64, size)
-                    scratch[3 * i][pl.ds(at, size), :] = pieces[n][first + i - base, :, t * 128 : (t + 1) * 128]
+    steps = mixed_ref.shape[0] // unroll
+
+    @pl.loop(0, steps)
+    def sectors(step):
+        first = step * unroll
+        for (k, base), piece in zip(layout, pieces):
+            length, size = piece.shape[:2]
+            start = 0 if k is None else (lax.axis_index("mom") ^ k) * size
+
+            def place(piece=piece, base=base, size=size, start=start):
+                for i in range(unroll):
+                    for t in range(pairs):
+                        at = pl.multiple_of(start + t * 64, size)
+                        scratch[3 * i][pl.ds(at, size), :] = piece[first + i - base, :, t * 128 : (t + 1) * 128]
+
+            if length == mixed_ref.shape[0]:
+                place()
+            else:
+                pl.when((first >= base) & (first < base + length))(place)
         for i in range(unroll):
             rs, res = scratch[3 * i : 3 * i + 2]
             even = jnp.dot(mixed_ref[first + i, 0], rs[...], preferred_element_type=F32)
@@ -199,9 +209,6 @@
                     for k in range(4):
                         fin[t, pl.ds(k, 16, stride=4), :] = z[k * 16 : (k + 1) * 16]
                     outs[0][first + i, :, cols] = fin[t]
-
-    for lo, hi, parts in spans:
-        pl.loop(0, (hi - lo) // unroll)(functools.partial(sectors, parts, lo))
 
 
 def combine_kernel(dims_ref, turn_ref, shifted_ref, *refs):
@@ -287,16 +294,12 @@
 
 def close(mixed, pieces, direct):
     lanes, sectors = pieces[0][0].shape[2], mixed.shape[0]
-    cuts = sorted({0, sectors} | {lo for _, _, lo in pieces})
-    spans = []
-    for lo, hi in zip(cuts, cuts[1:]):
-        parts = [(n, k, base) for n, (p, k, base) in enumerate(pieces) if base <= lo and hi <= base + p.shape[0]]
-        spans.append((lo, hi, parts))
+    layout = [(k, base) for _, k, base in pieces]
     rows, kind, count = (16, BF16, 4) if direct else (64, F32, 1)
-    unroll = UNROLL if all((hi - lo) % UNROLL == 0 for lo, hi, _ in spans) else 1
+    unroll = UNROLL if all(p.shape[0] % UNROLL == 0 for p, _, _ in pieces) and sectors > UNROLL else 1
     vmem = pl.BlockSpec(memory_space=pltpu.VMEM)
     return pl.pallas_call(
-        functools.partial(close_kernel, lanes // 128, spans, direct, len(pieces), unroll),
+        functools.partial(close_kernel, lanes // 128, layout, direct, unroll),
         in_specs=[vmem] * (1 + len(pieces)),
         out_specs=[vmem] * count,
         out_shape=[jax.ShapeDtypeStruct((sectors, rows, 256), kind)] * count,

time: 61.8 us -> 60.9 us (0.985)
  Pallas kernels: 34 us -> 33.1 us
    pallas_call x2, Pallas kernels: 9.25 us -> 8.34 us  [close(): pl.pallas_call(functools.partial(close_kernel, lanes // 128, layout, dire...]
where the time goes in v4:
time: 60.9 us; the launch traced here: 60.5 us
  Pallas kernels  33.1 us (54%)
  starting transfers between devices  16.7 us (27%)
  local copies, waits for them, and re-layouts  4.86 us (8%)
  waiting for transfers between devices  3.21 us (5%)
  other arithmetic  1.81 us (3%)
  between operations  0.82 us (1%)
    pallas_call x1, Pallas kernels, mix_shifted(): pl.pallas_call(functools.partial(shifted_kernel, pairs), grid=(sectors,),...  12.3 us
    pallas_call x1, Pallas kernels, mix_direct(): pl.pallas_call(functools.partial(direct_kernel, pairs, rows, len(sources)...  10.9 us
    pallas_call x2, Pallas kernels, close(): pl.pallas_call(functools.partial(close_kernel, lanes // 128, layout, dire...  8.34 us
    unnamed x12, local copies, waits for them, and re-layouts  4.8 us
    ppermute x2, starting transfers between devices, shards(): right1, right2 = (hop[1](right_env), hop[2](right_env))  4.46 us
    ppermute x3, starting transfers between devices, shards(): parts = [parts[0]] + [hop[k](parts[k]) for k in (1, 2, 3)]  3.65 us
    ppermute x3, starting transfers between devices, shards(): sources = [own] + [hop[k](own) for k in (1, 2, 3)]  3.55 us
    ppermute x1, starting transfers between devices, shards(): before = lax.ppermute(stacked[:, sectors - 1:], 'sec', up)  3.03 us
  transfers between devices with their start and end apart: 12, of which 3 were waited for; matrix products, arithmetic and copies ran while one was open for 3% of the time, Pallas kernels for 45%

profile of v4, /device:TPU:0, one launch (start us, length us, event | category | flops | bytes accessed | tf_op | source)
XLA Modules:
  0.0 60.5 jit_solution(3206393598486686708)
XLA Ops:
  0.0 3.0 %collective-permute-start.3 = (bf16[8,16,2816]{2,1,0:T(8,128)(2,1)}, bf16[8,16,2816]{2,1,0:T(8,128)(2,1)S(1)}, u32[]{:S(2)}, u32[]{:S(2)}) collective-permute-start(bf16[8,16,2816]{2,1,0:T(8,128)(2,1)} %refs_0_.5), channel_id=1, source_target_pairs={{0,16},{8,24},{16,0},{24,8},{1,17},{9,25},{17,1},{25,9},{2,18},{10... | collective-permute-start | bytes 2162696 | tf_op jit(solution)/shard_map/ppermute | solution.py:344
  3.0 1.5 %collective-permute-start.2 = (bf16[8,16,2816]{2,1,0:T(8,128)(2,1)}, bf16[8,16,2816]{2,1,0:T(8,128)(2,1)S(1)}, u32[]{:S(2)}, u32[]{:S(2)}) collective-permute-start(bf16[8,16,2816]{2,1,0:T(8,128)(2,1)} %refs_0_.5), channel_id=1, source_target_pairs={{0,8},{8,0},{16,24},{24,16},{1,9},{9,1},{17,25},{25,17},{2,10},{10... | collective-permute-start | bytes 2162696 | tf_op jit(solution)/shard_map/ppermute | solution.py:344
  4.5 0.8 %pad_maximum_fusion.1 = (bf16[2,1,64,256]{3,2,1,0:T(8,128)(2,1)S(1)}, bf16[2,1,64,256]{3,2,1,0:T(8,128)(2,1)S(1)}) fusion(bf16[1,8,64,256]{3,2,1,0:T(8,128)(2,1)} %bitcast.5, bf16[1,8,64,256]{3,2,1,0:T(8,128)(2,1)} %param.11), kind=kLoop, calls=%fused_computation.1 | loop fusion | flops 65536 | bytes 655360 | tf_op jit(solution)/shard_map/stack | solution.py:338
  5.3 1.3 %collective-permute-start.1 = (bf16[2,1,64,256]{3,2,1,0:T(8,128)(2,1)S(1)}, bf16[2,1,64,256]{3,2,1,0:T(8,128)(2,1)S(1)}, u32[]{:S(2)}, u32[]{:S(2)}) collective-permute-start(bf16[2,1,64,256]{3,2,1,0:T(8,128)(2,1)S(1)} %get-tuple-element.17), channel_id=1, source_target_pairs={{1,0},{2,1},{3,2},{4,3},{5,4},{6,5},{7,6},{9,8},{10,9},{11,10},{12... | collective-permute-start | bytes 196616 | tf_op jit(solution)/shard_map/ppermute | solution.py:340
  6.6 3.0 %collective-permute-start = (bf16[2,1,64,256]{3,2,1,0:T(8,128)(2,1)S(1)}, bf16[2,1,64,256]{3,2,1,0:T(8,128)(2,1)S(1)}, u32[]{:S(2)}, u32[]{:S(2)}) collective-permute-start(bf16[2,1,64,256]{3,2,1,0:T(8,128)(2,1)S(1)} %get-tuple-element.18), channel_id=1, source_target_pairs={{0,1},{1,2},{2,3},{3,4},{4,5},{5,6},{6,7},{8,9},{9,10},{10,11},{11... | collective-permute-start | bytes 196616 | tf_op jit(solution)/shard_map/ppermute | solution.py:339
  9.6 0.0 collective-permute-done.1.after_ref
  9.6 0.9 %collective-permute-done.before_ref = bf16[2,1,64,256]{3,2,1,0:T(8,128)(2,1)S(1)} collective-permute-done((bf16[2,1,64,256]{3,2,1,0:T(8,128)(2,1)S(1)}, bf16[2,1,64,256]{3,2,1,0:T(8,128)(2,1)S(1)}, u32[]{:S(2)}, u32[]{:S(2)}) %collective-permute-start) | collective-permute-done | bytes 65568 | tf_op jit(solution)/shard_map/ppermute | solution.py:339
  10.5 1.0 %pad_maximum_fusion.refs_1_.refs_5_.refs_9_ = bf16[1,10,64,256]{3,2,1,0:T(8,128)(2,1)S(1)} fusion(bf16[1,1,64,256]{3,2,1,0:T(8,128)(2,1)S(1)} %slice.27, bf16[1,8,64,256]{3,2,1,0:T(8,128)(2,1)} %param.11, bf16[1,1,64,256]{3,2,1,0:T(8,128)(2,1)S(1)} %slice.26), kind=kLoop, calls=%fused_computation | loop fusion | flops 327680 | bytes 655360 | tf_op jit(solution)/shard_map/concatenate | solution.py:341
  11.5 0.1 collective-permute-start.8
  11.6 2.0 %collective-permute-start.7 = (bf16[1,10,64,256]{3,2,1,0:T(8,128)(2,1)S(1)}, bf16[1,10,64,256]{3,2,1,0:T(8,128)(2,1)S(1)}, u32[]{:S(2)}, u32[]{:S(2)}) collective-permute-start(bf16[1,10,64,256]{3,2,1,0:T(8,128)(2,1)S(1)} %pad_maximum_fusion.refs_1_.refs_5_.refs_9_), channel_id=1, source_target_pairs={{0,16},{8,24},{16,0},{24,8},{1,17},{9,25},{17,1},{25,9},{2,18},{10... | collective-permute-start | bytes 983048 | tf_op jit(solution)/shard_map/ppermute | solution.py:345
  13.6 1.5 %collective-permute-start.6 = (bf16[1,10,64,256]{3,2,1,0:T(8,128)(2,1)S(1)}, bf16[1,10,64,256]{3,2,1,0:T(8,128)(2,1)S(1)}, u32[]{:S(2)}, u32[]{:S(2)}) collective-permute-start(bf16[1,10,64,256]{3,2,1,0:T(8,128)(2,1)S(1)} %pad_maximum_fusion.refs_1_.refs_5_.refs_9_), channel_id=1, source_target_pairs={{0,8},{8,0},{16,24},{24,16},{1,9},{9,1},{17,25},{25,17},{2,10},{10... | collective-permute-start | bytes 983048 | tf_op jit(solution)/shard_map/ppermute | solution.py:345
  15.7 0.0 copy-start
  15.7 0.9 %copy-done = bf16[8,64,256]{2,1,0:T(8,128)(2,1)S(1)} copy-done((bf16[8,64,256]{2,1,0:T(8,128)(2,1)S(1)}, bf16[8,64,256]{2,1,0:T(8,128)(2,1)}, u32[]{:S(2)}) %copy-start) | copy-done | bytes 262168
  16.7 0.0 copy-start.2
  16.7 1.8 %copy-done.2 = bf16[1,8,64,2816]{3,2,1,0:T(8,128)(2,1)S(1)} copy-done((bf16[1,8,64,2816]{3,2,1,0:T(8,128)(2,1)S(1)}, bf16[1,8,64,2816]{3,2,1,0:T(8,128)(2,1)}, u32[]{:S(2)}) %copy-start.2) | copy-done | bytes 2883608
  18.5 0.0 copy-start.3
  18.5 0.9 %copy-done.3 = bf16[44,4,44,4]{2,3,1,0:T(4,128)(2,1)S(1)} copy-done((bf16[44,4,44,4]{2,3,1,0:T(4,128)(2,1)S(1)}, bf16[44,4,44,4]{2,3,1,0:T(4,128)(2,1)}, u32[]{:S(2)}) %copy-start.3) | copy-done | bytes 61976
  19.4 12.3 %mix_shifted.1 = (bf16[8,2,256,1408]{3,2,1,0:T(8,128)(2,1)S(1)}, bf16[176,192]{1,0:T(8,128)(2,1)S(1)}) custom-call(bf16[8,64,2816]{2,1,0:T(8,128)(2,1)S(1)} %bitcast.6, bf16[8,64,256]{2,1,0:T(8,128)(2,1)S(1)} %copy-done, bf16[8,64,256]{2,1,0:T(8,128)(2,1)S(1)} %copy-done, bf16[8,64,256]{2,1,0:T(8,128)(2,1)S(1)} %copy-done, ...), custom_call_target="tpu_custom_call" | custom-call | flops 960000000 | bytes 1440000 | tf_op jit(solution)/shard_map/mix_shifted/pallas_call | solution.py:251
  31.7 0.0 collective-permute-done.3.refs_2_
  31.7 0.6 collective-permute-start.5
  32.3 0.0 collective-permute-done.2.refs_1_
  32.4 0.2 collective-permute-start.4
  32.5 0.0 collective-permute-done.8.refs_4_.refs_8_.refs_12_
  32.5 0.8 %collective-permute-done.7.refs_3_.refs_7_.refs_11_ = bf16[1,10,64,256]{3,2,1,0:T(8,128)(2,1)S(1)} collective-permute-done((bf16[1,10,64,256]{3,2,1,0:T(8,128)(2,1)S(1)}, bf16[1,10,64,256]{3,2,1,0:T(8,128)(2,1)S(1)}, u32[]{:S(2)}, u32[]{:S(2)}) %collective-permute-start.7) | collective-permute-done | bytes 327712 | tf_op jit(solution)/shard_map/ppermute | solution.py:345
  33.4 1.5 %collective-permute-done.6.refs_2_.refs_6_.refs_10_ = bf16[1,10,64,256]{3,2,1,0:T(8,128)(2,1)S(1)} collective-permute-done((bf16[1,10,64,256]{3,2,1,0:T(8,128)(2,1)S(1)}, bf16[1,10,64,256]{3,2,1,0:T(8,128)(2,1)S(1)}, u32[]{:S(2)}, u32[]{:S(2)}) %collective-permute-start.6) | collective-permute-done | bytes 327712 | tf_op jit(solution)/shard_map/ppermute | solution.py:345
  34.9 0.0 copy-start.5
  34.9 1.1 %copy-done.5 = bf16[8,16,2816]{2,1,0:T(8,128)(2,1)S(1)} copy-done((bf16[8,16,2816]{2,1,0:T(8,128)(2,1)S(1)}, bf16[8,16,2816]{2,1,0:T(8,128)(2,1)}, u32[]{:S(2)}) %copy-start.5) | copy-done | bytes 720920
  36.0 0.0 copy-start.1
  36.0 10.9 %mix_direct.1.mixed_ref = bf16[8,2,256,1408]{3,2,1,0:T(8,128)(2,1)S(1)} custom-call(bf16[8,16,2816]{2,1,0:T(8,128)(2,1)S(1)} %copy-done.5, bf16[1,10,64,256]{3,2,1,0:T(8,128)(2,1)S(1)} %pad_maximum_fusion.refs_1_.refs_5_.refs_9_, bf16[1,10,64,256]{3,2,1,0:T(8,128)(2,1)S(1)} %collective-permute-done.6.refs_2_.refs_6_.refs_10_, ...), custom_call_target="tpu_custom_call" | custom-call | flops 9600000000 | bytes 14400000 | tf_op jit(solution)/shard_map/mix_direct/pallas_call | solution.py:277
  46.9 0.0 copy-start.4
  46.9 0.0 collective-permute-done.5.refs_4_
  46.9 0.0 collective-permute-done.4.refs_3_
  46.9 0.0 copy-done.1
  46.9 4.1 %close_direct.1 = (bf16[8,16,256]{2,1,0:T(8,128)(2,1)S(1)}, bf16[8,16,256]{2,1,0:T(8,128)(2,1)S(1)}, bf16[8,16,256]{2,1,0:T(8,128)(2,1)S(1)}, bf16[8,16,256]{2,1,0:T(8,128)(2,1)S(1)}) custom-call(bf16[8,2,256,1408]{3,2,1,0:T(8,128)(2,1)S(1)} %mix_direct.1.mixed_ref, bf16[8,16,2816]{2,1,0:T(8,128)(2,1)S(1)} %copy-done.1, ...), custom_call_target="tpu_custom_call" | custom-call | flops 2400000000 | bytes 14400000 | tf_op jit(solution)/shard_map/close_direct/pallas_call | solution.py:301
  51.1 2.1 %collective-permute-start.9 = (bf16[8,16,256]{2,1,0:T(8,128)(2,1)S(1)}, bf16[8,16,256]{2,1,0:T(8,128)(2,1)S(1)}, u32[]{:S(2)}, u32[]{:S(2)}) collective-permute-start(bf16[8,16,256]{2,1,0:T(8,128)(2,1)S(1)} %get-tuple-element.14), channel_id=1, source_target_pairs={{0,8},{8,0},{16,24},{24,16},{1,9},{9,1},{17,25},{25,17},{2,10},{10... | collective-permute-start | bytes 196616 | tf_op jit(solution)/shard_map/ppermute | solution.py:357
  53.2 0.5 collective-permute-start.10
  53.7 1.0 %collective-permute-start.11 = (bf16[8,16,256]{2,1,0:T(8,128)(2,1)S(1)}, bf16[8,16,256]{2,1,0:T(8,128)(2,1)S(1)}, u32[]{:S(2)}, u32[]{:S(2)}) collective-permute-start(bf16[8,16,256]{2,1,0:T(8,128)(2,1)S(1)} %get-tuple-element.16), channel_id=1, source_target_pairs={{0,24},{8,16},{16,8},{24,0},{1,25},{9,17},{17,9},{25,1},{2,26},{10... | collective-permute-start | bytes 196616 | tf_op jit(solution)/shard_map/ppermute | solution.py:357
  54.7 4.2 %close_shifted.1.shifted_ref = f32[8,64,256]{2,1,0:T(8,128)S(1)} custom-call(bf16[8,2,256,1408]{3,2,1,0:T(8,128)(2,1)S(1)} %get-tuple-element.11.mixed_ref, bf16[8,16,2816]{2,1,0:T(8,128)(2,1)S(1)} %copy-done.1, bf16[8,16,2816]{2,1,0:T(8,128)(2,1)S(1)} %collective-permute-done.2.refs_1_, bf16[8,16,2816]{2,1,0:T(8,128)(2,1)S(1)} %collective-permute-done.3.refs_2_, ...), custom_call_target="tpu_custom_call" | custom-call | flops 2400000000 | bytes 14400000 | tf_op jit(solution)/shard_map/close_shifted/pallas_call | solution.py:301
  58.9 0.0 collective-permute-done.9.refs_1_
  58.9 0.0 collective-permute-done.10.refs_2_
  58.9 0.0 collective-permute-done.11.refs_3_
  59.0 0.0 copy-done.4
  59.0 1.6 %combine.1 = bf16[1,2,8,64,256]{4,3,2,1,0:T(8,128)(2,1)} custom-call(s32[8]{0:T(128)S(1)} %copy-done.4, f32[1]{0:T(128)S(6)} %div.3.turn_ref, f32[8,64,256]{2,1,0:T(8,128)S(1)} %close_shifted.1.shifted_ref, bf16[8,16,256]{2,1,0:T(8,128)(2,1)S(1)} %get-tuple-element.13.refs_0_, bf16[8,16,256]{2,1,0:T(8,128)(2,1)S(1)} %collective-permute-done.9.refs_1_, ...), custom_call_target="tpu_custom_call" | custom-call | flops 800000 | bytes 1600000 | tf_op jit(solution)/shard_map/combine/pallas_call | solution.py:316
  (4 shorter events, 0.1 us)
Async XLA Ops:
  0.0 31.7 %collective-permute-start.3 = (bf16[8,16,2816]{2,1,0:T(8,128)(2,1)}, bf16[8,16,2816]{2,1,0:T(8,128)(2,1)S(1)}, u32[]{:S(2)}, u32[]{:S(2)}) collective-permute-start(bf16[8,16,2816]{2,1,0:T(8,128)(2,1)} %refs_0_.5), channel_id=1, source_target_pairs={{0,16},{8,24},{16,0},{24,8},{1,17},{9,25},{17,1},{25,9},{2,18},{10... | collective-permute-start | bytes 2162696 | tf_op jit(solution)/shard_map/ppermute | solution.py:344
  3.0 29.4 %collective-permute-start.2 = (bf16[8,16,2816]{2,1,0:T(8,128)(2,1)}, bf16[8,16,2816]{2,1,0:T(8,128)(2,1)S(1)}, u32[]{:S(2)}, u32[]{:S(2)}) collective-permute-start(bf16[8,16,2816]{2,1,0:T(8,128)(2,1)} %refs_0_.5), channel_id=1, source_target_pairs={{0,8},{8,0},{16,24},{24,16},{1,9},{9,1},{17,25},{25,17},{2,10},{10... | collective-permute-start | bytes 2162696 | tf_op jit(solution)/shard_map/ppermute | solution.py:344
  5.3 4.3 %collective-permute-start.1 = (bf16[2,1,64,256]{3,2,1,0:T(8,128)(2,1)S(1)}, bf16[2,1,64,256]{3,2,1,0:T(8,128)(2,1)S(1)}, u32[]{:S(2)}, u32[]{:S(2)}) collective-permute-start(bf16[2,1,64,256]{3,2,1,0:T(8,128)(2,1)S(1)} %get-tuple-element.17), channel_id=1, source_target_pairs={{1,0},{2,1},{3,2},{4,3},{5,4},{6,5},{7,6},{9,8},{10,9},{11,10},{12... | collective-permute-start | bytes 196616 | tf_op jit(solution)/shard_map/ppermute | solution.py:340
  6.6 3.9 %collective-permute-start = (bf16[2,1,64,256]{3,2,1,0:T(8,128)(2,1)S(1)}, bf16[2,1,64,256]{3,2,1,0:T(8,128)(2,1)S(1)}, u32[]{:S(2)}, u32[]{:S(2)}) collective-permute-start(bf16[2,1,64,256]{3,2,1,0:T(8,128)(2,1)S(1)} %get-tuple-element.18), channel_id=1, source_target_pairs={{0,1},{1,2},{2,3},{3,4},{4,5},{5,6},{6,7},{8,9},{9,10},{10,11},{11... | collective-permute-start | bytes 196616 | tf_op jit(solution)/shard_map/ppermute | solution.py:339
  11.5 21.0 %collective-permute-start.8 = (bf16[1,10,64,256]{3,2,1,0:T(8,128)(2,1)S(1)}, bf16[1,10,64,256]{3,2,1,0:T(8,128)(2,1)S(1)}, u32[]{:S(2)}, u32[]{:S(2)}) collective-permute-start(bf16[1,10,64,256]{3,2,1,0:T(8,128)(2,1)S(1)} %pad_maximum_fusion.refs_1_.refs_5_.refs_9_), channel_id=1, source_target_pairs={{0,24},{8,16},{16,8},{24,0},{1,25},{9,17},{17,9},{25,1},{2,26},{10... | collective-permute-start | bytes 983048 | tf_op jit(solution)/shard_map/ppermute | solution.py:345
  11.6 21.8 %collective-permute-start.7 = (bf16[1,10,64,256]{3,2,1,0:T(8,128)(2,1)S(1)}, bf16[1,10,64,256]{3,2,1,0:T(8,128)(2,1)S(1)}, u32[]{:S(2)}, u32[]{:S(2)}) collective-permute-start(bf16[1,10,64,256]{3,2,1,0:T(8,128)(2,1)S(1)} %pad_maximum_fusion.refs_1_.refs_5_.refs_9_), channel_id=1, source_target_pairs={{0,16},{8,24},{16,0},{24,8},{1,17},{9,25},{17,1},{25,9},{2,18},{10... | collective-permute-start | bytes 983048 | tf_op jit(solution)/shard_map/ppermute | solution.py:345
  13.6 21.3 %collective-permute-start.6 = (bf16[1,10,64,256]{3,2,1,0:T(8,128)(2,1)S(1)}, bf16[1,10,64,256]{3,2,1,0:T(8,128)(2,1)S(1)}, u32[]{:S(2)}, u32[]{:S(2)}) collective-permute-start(bf16[1,10,64,256]{3,2,1,0:T(8,128)(2,1)S(1)} %pad_maximum_fusion.refs_1_.refs_5_.refs_9_), channel_id=1, source_target_pairs={{0,8},{8,0},{16,24},{24,16},{1,9},{9,1},{17,25},{25,17},{2,10},{10... | collective-permute-start | bytes 983048 | tf_op jit(solution)/shard_map/ppermute | solution.py:345
  15.7 1.0 %copy-start = (bf16[8,64,256]{2,1,0:T(8,128)(2,1)S(1)}, bf16[8,64,256]{2,1,0:T(8,128)(2,1)}, u32[]{:S(2)}) copy-start(bf16[8,64,256]{2,1,0:T(8,128)(2,1)} %s2_ref.1) | copy-start | bytes 786436
  16.7 1.8 %copy-start.2 = (bf16[1,8,64,2816]{3,2,1,0:T(8,128)(2,1)S(1)}, bf16[1,8,64,2816]{3,2,1,0:T(8,128)(2,1)}, u32[]{:S(2)}) copy-start(bf16[1,8,64,2816]{3,2,1,0:T(8,128)(2,1)} %param.10) | copy-start | bytes 8650756
  18.5 0.9 %copy-start.3 = (bf16[44,4,44,4]{2,3,1,0:T(4,128)(2,1)S(1)}, bf16[44,4,44,4]{2,3,1,0:T(4,128)(2,1)}, u32[]{:S(2)}) copy-start(bf16[44,4,44,4]{2,3,1,0:T(4,128)(2,1)} %param.13) | copy-start | bytes 185860
  31.7 15.2 %collective-permute-start.5 = (bf16[4,16,2816]{2,1,0:T(8,128)(2,1)S(1)}, bf16[4,16,2816]{2,1,0:T(8,128)(2,1)S(1)}, u32[]{:S(2)}, u32[]{:S(2)}) collective-permute-start(bf16[4,16,2816]{2,1,0:T(8,128)(2,1)S(1)} %slice.25), channel_id=1, source_target_pairs={{0,8},{8,0},{16,24},{24,16},{1,9},{9,1},{17,25},{25,17},{2,10},{10... | collective-permute-start | bytes 1081352 | tf_op jit(solution)/shard_map/ppermute | solution.py:346
  32.4 14.5 %collective-permute-start.4 = (bf16[4,16,2816]{2,1,0:T(8,128)(2,1)S(1)}, bf16[4,16,2816]{2,1,0:T(8,128)(2,1)S(1)}, u32[]{:S(2)}, u32[]{:S(2)}) collective-permute-start(bf16[4,16,2816]{2,1,0:T(8,128)(2,1)S(1)} %slice.24), channel_id=1, source_target_pairs={{0,16},{8,24},{16,0},{24,8},{1,17},{9,25},{17,1},{25,9},{2,18},{10... | collective-permute-start | bytes 1081352 | tf_op jit(solution)/shard_map/ppermute | solution.py:346
  34.9 1.1 %copy-start.5 = (bf16[8,16,2816]{2,1,0:T(8,128)(2,1)S(1)}, bf16[8,16,2816]{2,1,0:T(8,128)(2,1)}, u32[]{:S(2)}) copy-start(bf16[8,16,2816]{2,1,0:T(8,128)(2,1)} %refs_0_.4) | copy-start | bytes 2162692
  36.0 10.9 %copy-start.1 = (bf16[8,16,2816]{2,1,0:T(8,128)(2,1)S(1)}, bf16[8,16,2816]{2,1,0:T(8,128)(2,1)}, u32[]{:S(2)}) copy-start(bf16[8,16,2816]{2,1,0:T(8,128)(2,1)} %refs_0_.5) | copy-start | bytes 2162692
  46.9 12.1 %copy-start.4 = (s32[8]{0:T(128)S(1)}, s32[8]{0:T(128)}, u32[]{:S(2)}) copy-start(s32[8]{0:T(128)} %dims_ref.1) | copy-start | bytes 100
  51.1 7.9 %collective-permute-start.9 = (bf16[8,16,256]{2,1,0:T(8,128)(2,1)S(1)}, bf16[8,16,256]{2,1,0:T(8,128)(2,1)S(1)}, u32[]{:S(2)}, u32[]{:S(2)}) collective-permute-start(bf16[8,16,256]{2,1,0:T(8,128)(2,1)S(1)} %get-tuple-element.14), channel_id=1, source_target_pairs={{0,8},{8,0},{16,24},{24,16},{1,9},{9,1},{17,25},{25,17},{2,10},{10... | collective-permute-start | bytes 196616 | tf_op jit(solution)/shard_map/ppermute | solution.py:357
  53.2 5.8 %collective-permute-start.10 = (bf16[8,16,256]{2,1,0:T(8,128)(2,1)S(1)}, bf16[8,16,256]{2,1,0:T(8,128)(2,1)S(1)}, u32[]{:S(2)}, u32[]{:S(2)}) collective-permute-start(bf16[8,16,256]{2,1,0:T(8,128)(2,1)S(1)} %get-tuple-element.15), channel_id=1, source_target_pairs={{0,16},{8,24},{16,0},{24,8},{1,17},{9,25},{17,1},{25,9},{2,18},{10... | collective-permute-start | bytes 196616 | tf_op jit(solution)/shard_map/ppermute | solution.py:357
  53.7 5.3 %collective-permute-start.11 = (bf16[8,16,256]{2,1,0:T(8,128)(2,1)S(1)}, bf16[8,16,256]{2,1,0:T(8,128)(2,1)S(1)}, u32[]{:S(2)}, u32[]{:S(2)}) collective-permute-start(bf16[8,16,256]{2,1,0:T(8,128)(2,1)S(1)} %get-tuple-element.16), channel_id=1, source_target_pairs={{0,24},{8,16},{16,8},{24,0},{1,25},{9,17},{17,9},{25,1},{2,26},{10... | collective-permute-start | bytes 196616 | tf_op jit(solution)/shard_map/ppermute | solution.py:357
